TPU v7x, 32 devices: a whole 2x2x4 slice. The times are simulated.
32 devices in a mesh: dp: 8 (over y, x, core), tp: 4 (over z).
Axes of the slice: x: 2, y: 2, z: 4, core: 2. Of those that a mesh axis runs over, the one named last changes fastest.
Arguments:
- inputs: bfloat16 [26624, 768], P(('dp', 'tp')), may hold values from -6 to 6
- segment_ids: int32 [32, 832], P('dp'), may hold values from -1 to 4, as said below
- mask_flags: int32 [32, 832], P(('dp', 'tp')), may hold values 0 or 1
- mask_token: bfloat16 [768], replicated, may hold values from -6 to 6
- norm_gain: bfloat16 [768], replicated, may hold values from 0.5 to 1.5
- norm_shift: bfloat16 [768], replicated, may hold values from -3 to 3
- heads_weight: bfloat16 [768, 12, 192], P(None, 'tp'), may hold values from -0.21875 to 0.21875
- heads_bias: bfloat16 [12, 128], P('tp'), may hold values from -1.1953125 to 1.1953125
- proj_weight: bfloat16 [768, 768], P('tp'), may hold values from -1.75 to 1.75
- proj_bias: bfloat16 [768], replicated, may hold values from -2 to 2
- attn_scale: bfloat16 [768], replicated, may hold values from 0.5 to 1.5
- mlp_gain: bfloat16 [768], replicated, may hold values from 0.5 to 1.5
- mlp_shift: bfloat16 [768], replicated, may hold values from -3 to 3
- up_weight: bfloat16 [768, 3072], P(None, 'tp'), may hold values from -0.21875 to 0.21875
- up_bias: bfloat16 [3072], P('tp'), may hold values from -2 to 2
- down_weight: bfloat16 [3072, 768], P('tp'), may hold values from -0.109375 to 0.109375
- down_bias: bfloat16 [768], replicated, may hold values from -2 to 2
- mlp_scale: bfloat16 [768], replicated, may hold values from 0.5 to 1.5
- grad_out: bfloat16 [26624, 768], P(('dp', 'tp')), may hold values from -6 to 6
Outputs:
- output: bfloat16 [26624, 768], P(('dp', 'tp'))
- grad_inputs: float32 [26624, 768], P(('dp', 'tp'))
- grad_token: float32 [768], replicated
- grad_norm_gain: float32 [768], replicated
- grad_norm_shift: float32 [768], replicated
- grad_heads_weight: float32 [768, 12, 192], P(None, 'tp')
- grad_heads_bias: float32 [12, 128], P('tp')
- grad_proj_weight: float32 [768, 768], P('tp')
- grad_proj_bias: float32 [768], replicated
- grad_attn_scale: float32 [768], replicated
- grad_mlp_gain: float32 [768], replicated
- grad_mlp_shift: float32 [768], replicated
- grad_up_weight: float32 [768, 3072], P(None, 'tp')
- grad_up_bias: float32 [3072], P('tp')
- grad_down_weight: float32 [3072, 768], P('tp')
- grad_down_bias: float32 [768], replicated
- grad_mlp_scale: float32 [768], replicated
Inputs may be any that keep to these rules, and one draw needn't show every extreme that they name: `segment_ids`: every packed row holds five images numbered 0 to 4 in order from its first slot, then 1 to 32 padding slots marked -1 at its end; each of the first four images has h * w + 1 slots with h and w from 11 to 14, the fifth fills the rest.
All inputs are finite; a program needn't handle non-finite values. No bound on the sum of `mask_flags` on one device may be relied on, other than what follows from the above.
Results may differ from a plain program's by a relative error of at most 0.02.
Values may be sent and summed in bfloat16 or wider, within the bound.
A program may use at most 192 MiB of HBM per device.

v0:
```python
import functools

import jax
import jax.numpy as jnp
from jax import lax
from jax.experimental import pallas as pl
from jax.experimental.pallas import tpu as pltpu
from jax.sharding import PartitionSpec as P

EPSILON = 1e-06
FLOOR_SCORE = -1e30
SQRT_HALF = 0.7071067811865476
INV_ROOT_TWO_PI = 0.3989422804014327
LONGEST = 14 * 14 + 1
FIFTH_FROM = 4 * (11 * 11 + 1)
TILE = 128
CORE, X, Y = 1, 2, 4

f32, bf16 = jnp.float32, jnp.bfloat16
NN = (((1,), (0,)), ((), ()))
NT = (((1,), (1,)), ((), ()))
TN = (((0,), (0,)), ((), ()))


def dot(a, b, dims=NN):
    return lax.dot_general(a, b, dims, preferred_element_type=f32)


def layer_norm(values, gain, shift):
    centre = values - jnp.mean(values, axis=-1, keepdims=True)
    inverse = lax.rsqrt(jnp.mean(centre * centre, axis=-1, keepdims=True) + EPSILON)
    scaled = centre * inverse
    return (scaled * gain + shift, scaled, inverse)


def norm_back(grad_normed, scaled, inverse, gain):
    grad_scaled = grad_normed * gain
    first = jnp.mean(grad_scaled, axis=-1, keepdims=True)
    second = jnp.mean(grad_scaled * scaled, axis=-1, keepdims=True)
    return inverse * (grad_scaled - first - scaled * second)


def gelu_parts(inner):
    normal_cdf = 0.5 * (1.0 + lax.erf(inner * SQRT_HALF))
    density = jnp.exp(-0.5 * inner * inner) * INV_ROOT_TWO_PI
    return (inner * normal_cdf, normal_cdf + inner * density)


def head_bias_row(bias, head_size):
    blank = jnp.zeros((bias.shape[0], head_size), f32)
    joined = jnp.concatenate(
        [bias[:, :head_size].astype(f32), blank, bias[:, head_size:].astype(f32)], axis=1
    )
    return joined.reshape(1, -1)


def exchange(value, dp_bits=0, tp_bits=0):
    n_dp, n_tp = lax.axis_size("dp"), lax.axis_size("tp")
    pairs = [
        (d * n_tp + t, (d ^ dp_bits) * n_tp + (t ^ tp_bits)) for d in range(n_dp) for t in range(n_tp)
    ]
    return lax.ppermute(value, ("dp", "tp"), pairs)


def windows(slots):
    out = []
    for low in range(0, slots, TILE):
        high = min(low + TILE, slots)
        begin = low - LONGEST + 1
        if low >= FIFTH_FROM:
            begin = min(begin, FIFTH_FROM)
        end = high + LONGEST - 1
        if high > FIFTH_FROM:
            end = slots
        begin = max(begin, 0) // 128 * 128
        end = min((end + 127) // 128 * 128, slots)
        out.append((low, high, begin, end))
    return out


def as_row(column):
    rows = column.shape[0]
    shape = (rows, rows)
    here = lax.broadcasted_iota(jnp.int32, shape, 0) == lax.broadcasted_iota(jnp.int32, shape, 1)
    return jnp.sum(jnp.where(here, column, 0.0), axis=0, keepdims=True)


def whole(*shape):
    return pl.BlockSpec(shape, lambda k: (0,) * len(shape))


def each(*shape, at=lambda k: k):
    return pl.BlockSpec((1,) + shape, lambda k: (at(k),) + (0,) * len(shape))


def params(megabytes):
    return pltpu.CompilerParams(vmem_limit_bytes=megabytes << 20)


def cost(flops, moved, exps=0):
    return pl.CostEstimate(flops=int(flops), transcendentals=int(exps), bytes_accessed=int(moved))


def start_of(inputs_ref, column_ref, flag_ref, token_ref, here):
    valid = (column_ref[here, :] >= 0).astype(f32)
    flagged = (flag_ref[here, :] == 1).astype(f32)
    start = valid * (flagged * token_ref[...].astype(f32) + (1.0 - flagged) * inputs_ref[here, :].astype(f32))
    return valid, flagged, start


def rows_of(slots, step=104):
    return [(low, min(low + step, slots)) for low in range(0, slots, step)]


def flip(index, bits):
    bit = 1
    while bit <= bits:
        if bits & bit:
            index = index + bit * (1 - 2 * lax.rem(lax.div(index, bit), 2))
        bit *= 2
    return index


class Gather:
    ROUTES = ("z", "x", "y", "fx", "fy", "c0", "c2", "c4", "c6")
    COPIES = 3 * len(ROUTES)

    def __init__(self, shard_ref, full_ref, send_sems, recv_sems):
        self.dp, self.tp = lax.axis_index("dp"), lax.axis_index("tp")
        self.own = lax.rem(self.dp, 8)
        self.shard, self.full = shard_ref, full_ref
        self.sends, self.recvs = send_sems, recv_sems
        self.rows = shard_ref.shape[0] // 8
        self.half = self.rows // 16 * 8

    def piece(self, k, bits, half=None):
        begin, height = flip(self.own, bits) * self.rows, self.rows
        if half == 0:
            height = self.half
        elif half == 1:
            begin, height = begin + self.half, self.rows - self.half
        return self.full.at[k, pl.ds(pl.multiple_of(begin, 8), height), :]

    def copy(self, k, route):
        if route == "z":
            source = self.shard.at[pl.ds(pl.multiple_of(self.own * self.rows, 8), self.rows), :]
            target, to = self.piece(k, 0), (self.dp, flip(self.tp, k))
        else:
            bits, half, link = {
                "x": (0, None, X), "y": (0, None, Y), "fx": (Y, 1, X), "fy": (X, 0, Y),
                "c0": (0, None, CORE), "c2": (X, None, CORE), "c4": (Y, None, CORE), "c6": (X | Y, None, CORE),
            }[route]
            source = target = self.piece(k, bits, half)
            to = (flip(self.dp, link), self.tp)
        n = (k - 1) * len(self.ROUTES) + self.ROUTES.index(route)
        return pltpu.make_async_remote_copy(
            src_ref=source, dst_ref=target, send_sem=self.sends.at[n], recv_sem=self.recvs.at[n],
            device_id=to, device_id_type=pl.DeviceIdType.MESH,
        )

    def start(self, k, *routes):
        for route in routes:
            self.copy(k, route).start()

    def arrived(self, k, *routes):
        for route in routes:
            self.copy(k, route).wait_recv()

    def begin(self, k):
        self.start(k, "z")

    def step1(self, k):
        self.arrived(k, "z")
        self.start(k, "x", "y", "c0")

    def step2(self, k):
        self.arrived(k, "x")
        self.start(k, "fy", "c2")
        self.arrived(k, "y")
        self.start(k, "fx", "c4")

    def step3(self, k):
        self.arrived(k, "fx", "fy")
        self.start(k, "c6")

    def step4(self, k):
        self.arrived(k, "c0", "c2", "c4", "c6")

    def sent(self):
        for k in (1, 2, 3):
            for route in self.ROUTES:
                self.copy(k, route).wait_send()


def meet(peers):
    barrier = pltpu.get_barrier_semaphore()
    for peer in peers:
        pl.semaphore_signal(barrier, inc=1, device_id=peer, device_id_type=pl.DeviceIdType.MESH)
    pl.semaphore_wait(barrier, len(peers))


def gather_attend_kernel(
    inputs_ref, column_ref, row_ref, flag_ref, token_ref, gain_ref, shift_ref, bias_ref,
    heads_ref, up_ref, proj_ref, down_ref,
    normed_ref, packed_ref, mixed_ref, lse_ref, heads_all, up_all, proj_all, down_all,
    weight, bounce_up, bounce_proj, bounce_down, load_sem, own_sems,
    *sems,
):
    slots = inputs_ref.shape[0]
    triple = weight.shape[1] // 3
    size = triple // 3
    scale = size ** (-0.5)
    step = pl.program_id(0)
    shards, fulls = (heads_ref, up_ref, proj_ref, down_ref), (heads_all, up_all, proj_all, down_all)
    heads, up, proj, down = gathers = [Gather(shards[n], fulls[n], sems[2 * n], sems[2 * n + 1]) for n in range(4)]
    bounces = (weight, bounce_up, bounce_proj, bounce_down)
    loads = [pltpu.make_async_copy(shards[n], bounces[n], own_sems.at[n]) for n in range(4)]
    stores = [pltpu.make_async_copy(bounces[n], fulls[n].at[0], own_sems.at[4 + n]) for n in range(4)]

    events = {}

    def on(at, unit, *actions):
        events.setdefault((at, unit), []).extend(actions)

    for k, (a, b, c) in {1: (3, 9, 14), 2: (14, 20, 23), 3: (16, 22, 25)}.items():
        for unit, action in ((a, heads.step1), (b, heads.step2), (c, heads.step3)):
            on(unit // 21, unit % 21, functools.partial(action, k))
    for n, item in enumerate((proj, up, down)):
        on(0, 6 if n < 2 else 16, *[functools.partial(item.begin, k) for k in (1, 2, 3)])
    for item, base in ((proj, 28), (up, 30), (down, 52)):
        for k in (1, 2, 3):
            for n, action in enumerate((item.step1, item.step2, item.step3)):
                unit = min(base + 3 * k + n * 14, 83)
                on(unit // 21, unit % 21, functools.partial(action, k))

    def pump(unit):
        for at in range(4):
            if (at, unit) in events:

                @pl.when(step == at)
                def _():
                    for action in events[(at, unit)]:
                        action()

    @pl.when(step == 0)
    def _():
        dp, tp = heads.dp, heads.tp
        loads[0].start()
        meet([(dp, flip(tp, k)) for k in (1, 2, 3)] + [(flip(dp, bit), tp) for bit in (X, Y, CORE)])
        for k in (1, 2, 3):
            heads.begin(k)
        for load in loads[1:]:
            load.start()
        gain, shift = gain_ref[...].astype(f32), shift_ref[...].astype(f32)
        for low, high in rows_of(slots):
            _, _, start = start_of(inputs_ref, column_ref, flag_ref, token_ref, slice(low, high))
            normed_ref[low:high, :] = layer_norm(start, gain, shift)[0].astype(bf16)
        loads[0].wait()
        stores[0].start()

    for k in (1, 2, 3):

        @pl.when(step == k)
        def _():
            if k == 1:
                stores[0].wait()
            heads.step4(k)
            load = pltpu.make_async_copy(heads_all.at[k], weight, load_sem)
            load.start()
            load.wait()

    for low in range(0, slots, 208):
        packed_ref[0, low:low + 208, :] = (dot(normed_ref[low:low + 208, :], weight[...]) + bias_ref[0]).astype(bf16)
    lse_ref[...] = jnp.zeros_like(lse_ref)
    unit = 0
    for head in range(3):
        base = head * triple
        for low, high, begin, end in windows(slots):
            query = packed_ref[0, low:high, base:base + size] * jnp.bfloat16(scale)
            keys = packed_ref[0, begin:end, base + size:base + 2 * size]
            values = packed_ref[0, begin:end, base + 2 * size:base + 3 * size]
            scores = dot(query, keys, NT)
            same = column_ref[low:high, :] == row_ref[:, begin:end]
            scores = jnp.where(same, scores, FLOOR_SCORE)
            largest = jnp.max(scores, axis=1, keepdims=True)
            raised = jnp.exp(scores - largest)
            total = jnp.sum(raised, axis=1, keepdims=True)
            mixed = dot(raised.astype(bf16), values) * (1.0 / total)
            mixed_ref[0, low:high, head * size:(head + 1) * size] = mixed.astype(bf16)
            lse_ref[0, head:head + 1, low:high] = as_row(largest + jnp.log(total))
            pump(unit)
            unit += 1

    @pl.when(step == 0)
    def _():
        for load, store in zip(loads[1:], stores[1:]):
            load.wait()
            store.start()

    @pl.when(step == 3)
    def _():
        for store in stores[1:]:
            store.wait()
        for item in (proj, up, down):
            for k in (1, 2, 3):
                item.step4(k)
        for item in gathers:
            item.sent()


def gather_attend(inputs, column, row, flag, token, gain, shift, bias, heads, up, proj, down):
    slots, width = inputs.shape
    columns = heads.shape[1]
    vector, anywhere = whole(1, width), pl.BlockSpec(memory_space=pl.ANY)
    sems = [pltpu.SemaphoreType.DMA((Gather.COPIES,))] * 8
    return pl.pallas_call(
        gather_attend_kernel,
        grid=(4,),
        in_specs=[
            whole(slots, width), whole(slots, 1), whole(1, slots), whole(slots, 1), vector, vector, vector,
            each(1, columns), anywhere, anywhere, anywhere, anywhere,
        ],
        out_specs=[
            whole(slots, width), each(slots, columns), each(slots, columns // 3), each(8, slots),
            anywhere, anywhere, anywhere, anywhere,
        ],
        out_shape=[
            jax.ShapeDtypeStruct((slots, width), bf16),
            jax.ShapeDtypeStruct((4, slots, columns), bf16),
            jax.ShapeDtypeStruct((4, slots, columns // 3), bf16),
            jax.ShapeDtypeStruct((4, 8, slots), f32),
        ] + [jax.ShapeDtypeStruct((4,) + item.shape, bf16) for item in (heads, up, proj, down)],
        scratch_shapes=[
            pltpu.VMEM(heads.shape, bf16), pltpu.VMEM(up.shape, bf16), pltpu.VMEM(proj.shape, bf16),
            pltpu.VMEM(down.shape, bf16), pltpu.SemaphoreType.DMA, pltpu.SemaphoreType.DMA((8,)),
        ] + sems,
        compiler_params=pltpu.CompilerParams(vmem_limit_bytes=40 << 20, collective_id=0, has_side_effects=True),
        cost_estimate=cost(16e9, 40e6, 12 * 480000),
        name="gather_attend",
    )(inputs, column, row, flag, token, gain, shift, bias, heads, up, proj, down)


def mlp_kernel(
    inputs_ref, column_ref, flag_ref, token_ref, mixed_ref, proj_ref, proj_bias_ref, attn_scale_ref,
    gain_ref, shift_ref, up_ref, unit_bias_ref, down_ref, down_bias_ref, mlp_scale_ref, grad_out_ref,
    middle_ref, normed_ref, hidden_ref, slope_ref, output_ref, grad_low_ref, sums_ref,
    mixed, total,
):
    slots = inputs_ref.shape[0]
    part = mixed_ref.shape[2]
    k = pl.program_id(0)

    @pl.when(k == 0)
    def _():
        for n in range(4):
            mixed[:, n * part:(n + 1) * part] = mixed_ref[n]
        proj_bias, attn_scale = proj_bias_ref[...].astype(f32), attn_scale_ref[...].astype(f32)
        gain, shift = gain_ref[...].astype(f32), shift_ref[...].astype(f32)
        for low, high in rows_of(slots, 208):
            _, _, start = start_of(inputs_ref, column_ref, flag_ref, token_ref, slice(low, high))
            branch1 = dot(mixed[low:high, :], proj_ref[...]) + proj_bias
            middle = start + attn_scale * branch1
            middle_ref[low:high, :] = middle
            normed_ref[low:high, :] = layer_norm(middle, gain, shift)[0].astype(bf16)
        total[...] = jnp.zeros_like(total)

    units = up_ref.shape[2]
    for low, high in rows_of(slots, 208):
        for left in range(0, units, 256):
            columns = slice(left, left + 256)
            inner = dot(normed_ref[low:high, :], up_ref[0, :, columns]) + unit_bias_ref[0, :, columns]
            value, slope = gelu_parts(inner)
            hidden_ref[0, low:high, columns] = value.astype(bf16)
            slope_ref[0, low:high, columns] = slope.astype(bf16)
        total[low:high, :] += dot(hidden_ref[0, low:high, :], down_ref[0])

    @pl.when(k == pl.num_programs(0) - 1)
    def _():
        down_bias, mlp_scale = down_bias_ref[...].astype(f32), mlp_scale_ref[...].astype(f32)
        sums_ref[...] = jnp.zeros_like(sums_ref)
        for low, high in rows_of(slots):
            valid = (column_ref[low:high, :] >= 0).astype(f32)
            branch2 = total[low:high, :] + down_bias
            output_ref[low:high, :] = (valid * (middle_ref[low:high, :] + mlp_scale * branch2)).astype(bf16)
            grad_final = valid * grad_out_ref[low:high, :].astype(f32)
            grad_branch2 = mlp_scale * grad_final
            grad_low_ref[low:high, :] = grad_branch2.astype(bf16)
            sums_ref[0:1, :] += jnp.sum(branch2 * grad_final, axis=0, keepdims=True)
            sums_ref[1:2, :] += jnp.sum(grad_branch2, axis=0, keepdims=True)


def mlp(inputs, column, flag, token, mixed, proj, proj_bias, attn_scale, gain, shift, up, unit_bias,
        down, down_bias, mlp_scale, grad_out):
    slots, width = inputs.shape
    count, _, units = up.shape
    vector = whole(1, width)
    tokens = whole(slots, width)
    return pl.pallas_call(
        mlp_kernel,
        grid=(count,),
        in_specs=[
            tokens, whole(slots, 1), whole(slots, 1), vector, whole(*mixed.shape),
            whole(width, width), vector, vector, vector, vector, each(width, units), each(1, units),
            each(units, width), vector, vector, tokens,
        ],
        out_specs=[
            tokens, tokens, each(slots, units), each(slots, units), tokens, tokens, whole(8, width),
        ],
        out_shape=[
            jax.ShapeDtypeStruct((slots, width), f32),
            jax.ShapeDtypeStruct((slots, width), bf16),
            jax.ShapeDtypeStruct((count, slots, units), bf16),
            jax.ShapeDtypeStruct((count, slots, units), bf16),
            jax.ShapeDtypeStruct((slots, width), bf16),
            jax.ShapeDtypeStruct((slots, width), bf16),
            jax.ShapeDtypeStruct((8, width), f32),
        ],
        scratch_shapes=[pltpu.VMEM((slots, width), bf16), pltpu.VMEM((slots, width), f32)],
        compiler_params=params(48),
        cost_estimate=cost(9e9, 30e6, 5e6),
        name="mlp",
    )(inputs, column, flag, token, mixed, proj, proj_bias, attn_scale, gain, shift, up, unit_bias,
      down, down_bias, mlp_scale, grad_out)


class Reduce:
    COPIES = 4 * 4 + 7

    def __init__(self, first, second, by_columns, keep, give, got, out, send_sems, recv_sems, own_sem):
        self.dp, self.tp = lax.axis_index("dp"), lax.axis_index("tp")
        self.first, self.second, self.by_columns = first, second, by_columns
        self.keep, self.give, self.out = keep, give, out
        self.got0, self.got1, self.got2, self.got_tp, self.total = got
        self.sends, self.recvs, self.own_sem = send_sems, recv_sems, own_sem
        self.rows, self.columns = keep.shape[1] * 2, keep.shape[2]
        self.bits = tuple(lax.rem(lax.div(self.dp, bit), 2) for bit in (CORE, first, second))

    def quarter(self, first):
        rows = self.rows // 4
        return pl.multiple_of(first * rows, 16), rows

    def eighth(self, first, second):
        begin, rows = self.quarter(first)
        if self.by_columns:
            width = self.columns // 2
            return begin, rows, pl.ds(pl.multiple_of(second * width, 128), width)
        return pl.multiple_of(begin + second * (rows // 2), 16), rows // 2, slice(None)

    def part(self, ref, spot):
        begin, rows, columns = spot
        return ref.at[pl.ds(begin, rows), columns]

    def place(self, flips):
        core, first, second = (1 - bit if turned else bit for bit, turned in zip(self.bits, flips))
        begin, rows, columns = self.eighth(first, second)
        return self.out.at[pl.ds(pl.multiple_of(core * (self.rows // 2) + begin, 16), rows), columns]

    def remote(self, n, source, target, bits=0, k=0):
        return pltpu.make_async_remote_copy(
            src_ref=source, dst_ref=target, send_sem=self.sends.at[n], recv_sem=self.recvs.at[n],
            device_id=(flip(self.dp, bits), flip(self.tp, k)), device_id_type=pl.DeviceIdType.MESH,
        )

    def copy(self, k, level):
        core, first, second = self.bits
        n = 4 * k + level
        if level == 0:
            return self.remote(n, self.give.at[k], self.got0.at[k], CORE)
        if level == 1:
            begin, rows = self.quarter(1 - first)
            return self.remote(n, self.keep.at[k, pl.ds(begin, rows), :], self.got1.at[k], self.first)
        if level == 2:
            return self.remote(n, self.part(self.keep.at[k], self.eighth(first, 1 - second)), self.got2.at[k], self.second)
        return self.remote(n, self.part(self.keep.at[k], self.eighth(first, second)), self.got_tp.at[k - 1], 0, k)

    def share(self, n):
        first, second = self.first, self.second
        bits, source = (
            (first, (0, 0, 0)), (second, (0, 0, 0)), (first | second, (0, 0, 0)), (CORE, (0, 0, 0)),
            (CORE, (0, 1, 0)), (CORE, (0, 0, 1)), (CORE, (0, 1, 1)),
        )[n]
        place = self.place(source)
        return self.remote(16 + n, self.total if n < 4 else place, place, bits)

    def add(self, target, begin, rows, columns, *items):
        step = 48

        def body(i, carry):
            here = pl.ds(pl.multiple_of(begin + i * step, 16), step)
            there = pl.ds(pl.multiple_of(i * step, 16), step)
            total = target[here, columns].astype(f32)
            for item in items:
                total += item[there, :].astype(f32)
            target[here, columns] = total.astype(bf16)
            return carry

        lax.fori_loop(0, rows // step, body, 0)

    def step0(self, k):
        self.copy(k, 0).start()

    def given(self, k):
        self.copy(k, 0).wait_send()

    def step1(self, k):
        self.copy(k, 0).wait_recv()
        self.add(self.keep.at[k], 0, self.rows // 2, slice(None), self.got0.at[k])
        self.copy(k, 1).start()

    def step2(self, k):
        self.copy(k, 1).wait_recv()
        begin, rows = self.quarter(self.bits[1])
        self.add(self.keep.at[k], begin, rows, slice(None), self.got1.at[k])
        self.copy(k, 2).start()

    def step3(self, k):
        self.copy(k, 2).wait_recv()
        self.add(self.keep.at[k], *self.eighth(*self.bits[1:]), self.got2.at[k])
        if k:
            self.copy(k, 3).start()

    def step4(self):
        for k in (1, 2, 3):
            self.copy(k, 3).wait_recv()
        begin, rows, columns = self.eighth(*self.bits[1:])
        self.add(self.keep.at[0], begin, rows, columns, *[self.got_tp.at[k] for k in range(3)])
        self.total[...] = self.keep[0, pl.ds(begin, rows), columns]
        for n in range(4):
            self.share(n).start()
        self.own_copy().start()

    def own_copy(self):
        return pltpu.make_async_copy(self.total, self.place((0, 0, 0)), self.own_sem)

    def step5(self):
        for n in range(3):
            self.share(n).wait_recv()
            self.share(4 + n).start()

    def step6(self, lowest=0):
        for n in range(3, 7):
            self.share(n).wait_recv()
        for n in range(7):
            self.share(n).wait_send()
        for k in range(4):
            for level in range(lowest, 4 if k else 3):
                self.copy(k, level).wait_send()
        self.own_copy().wait()


def schedule(points, events):
    table, rest = {}, []
    for when, action in sorted(events, key=lambda event: event[0]):
        key = next((key for key, time in points if time >= when), None)
        if key is None:
            rest.append(action)
        else:
            table.setdefault(key, []).append(action)
    return table, rest


VECTORS = 24
UNIT_ROW, HEAD_ROW = 9, 13


def back_kernel(
    grad_low_ref, hidden_ref, slope_ref, down_ref, up_ref, normed2_ref, middle_ref, grad_out_ref,
    inputs_ref, normed1_ref, packed_ref, mixed_ref, lse_ref, heads_ref, proj_ref, column_ref, row_ref, flag_ref,
    token_ref, gain1_ref, gain2_ref, attn_scale_ref, sums_ref,
    grad_inputs_ref, vector_ref, out_down, out_up, out_heads, out_proj,
    grad_unit, total, flipped, grad_mixed, grad_packed, delta, grad_query,
    keep_down, keep_up, keep_heads, keep_proj, give_down, give_heads, give_proj,
    vectors, vector_got, vector_tp, vector_sends, vector_recvs, own_sems,
    *rest,
):
    slots, width = normed2_ref.shape
    triple = heads_ref.shape[2] // 3
    size = triple // 3
    scale = size ** (-0.5)
    step = pl.program_id(0)
    got, sems = [rest[5 * n:5 * n + 5] for n in range(4)], rest[20:]
    give_up = give_down
    make = lambda n, first, second, by_columns, keep, give, out: Reduce(
        first, second, by_columns, keep, give, got[n], out, sems[2 * n], sems[2 * n + 1], own_sems.at[n])
    down = make(0, X, Y, False, keep_down, give_down, out_down)
    up = make(1, Y, X, False, keep_up, give_up, out_up)
    heads = make(2, X, Y, False, keep_heads, give_heads, out_heads)
    proj = make(3, Y, X, True, keep_proj, give_proj, out_proj)
    dp, tp, core = down.dp, down.tp, down.bits[0]
    n_dp = lax.axis_size("dp")
    levels = [bit for bit in (1, 2, 4, 8, 16, 32, 64, 128) if bit < n_dp]

    points = [((k, 0), 4.5 + 1.6 * k) for k in range(4)]
    points += [((4 + k, n), 10.5 + 6.4 * k + 1.2 * n) for k in range(4) for n in range(5)]
    points += [((8 + k, n), 40.0 + 13 * k + 0.5 * n) for k in range(4) for n in range(22)]
    points += [((12, n), 92.0 + n) for n in range(4)]
    events = []
    for k in range(4):
        events += [(8.5 + 1.6 * k, functools.partial(down.step1, k)), (17.0 + 6.5 * k, functools.partial(down.step2, k)),
                   (25.0 + 6.5 * k, functools.partial(down.step3, k))]
        events += [(19.5 + 6.4 * k, functools.partial(up.step1, k)), (30.0 + 7.0 * k, functools.partial(up.step2, k)),
                   (37.0 + 7.0 * k, functools.partial(up.step3, k))]
    events += [(53.0, down.step4), (63.0, down.step5), (68.0, up.step4), (79.0, up.step5)]
    for n, k in enumerate((1, 2, 3, 0)):
        done = 53.0 + 13 * n
        for item in (heads, proj):
            events += [(done + 3, functools.partial(item.step1, k)), (done + 10.5, functools.partial(item.step2, k)),
                       (done + 17, functools.partial(item.step3, k))]
    events += [(110.0, proj.step4), (110.1, heads.step4), (116.0, proj.step5), (116.1, heads.step5)]

    def vector_copy(n):
        if n < len(levels):
            return heads_like(vectors.at[n], vector_got.at[n], n, levels[n], 0)
        k = n - len(levels) + 1
        return heads_like(vectors.at[len(levels)], vector_tp.at[k - 1], n, 0, k)

    def heads_like(source, target, n, bits, k):
        return pltpu.make_async_remote_copy(
            src_ref=source, dst_ref=target, send_sem=vector_sends.at[n], recv_sem=vector_recvs.at[n],
            device_id=(flip(dp, bits), flip(tp, k)), device_id_type=pl.DeviceIdType.MESH,
        )

    def vector_step(n):
        vector_copy(n).wait_recv()
        vectors[n + 1] = vectors[n] + vector_got[n]
        if n + 1 < len(levels):
            vector_copy(n + 1).start()
        else:
            for k in (1, 2, 3):
                vector_copy(len(levels) + k - 1).start()

    events += [(99.0 + 3 * n, functools.partial(vector_step, n)) for n in range(len(levels))]
    table, tail = schedule(points, events)

    def pump(steps, unit):
        for at in steps:
            if (at, unit) in table:

                @pl.when(step == at)
                def _():
                    for action in table[(at, unit)]:
                        action()

    def each_send(item, place, steps):
        for k, at in steps:

            @pl.when(step == at)
            def _():
                item.step0(k)

    halves_of = (pl.ds(pl.multiple_of(core * (width // 2), 128), width // 2),
                 pl.ds(pl.multiple_of((1 - core) * (width // 2), 128), width // 2))

    @pl.when(step == 0)
    def _():
        vectors[0] = jnp.zeros_like(vectors[0])
        vectors[0, 7:8, :] = sums_ref[1:2, :]
        vectors[0, 8:9, :] = sums_ref[0:1, :]
        peers = [(dp, flip(tp, k)) for k in (1, 2, 3)]
        peers += [(flip(dp, bits), tp) for bits in (X, Y, X | Y, CORE)]
        peers += [(flip(dp, bit), tp) for bit in levels if bit >= 8]
        meet(peers)

    @pl.when(step < 4)
    def _():
        keep_down[step] = dot(hidden_ref[0, :, halves_of[0]], grad_low_ref[...], TN).astype(bf16)
        give_down[step] = dot(hidden_ref[0, :, halves_of[1]], grad_low_ref[...], TN).astype(bf16)
        each_send(down, 0, [(k, k) for k in range(4)])
        pump(range(4), 0)

    @pl.when(step == 4)
    def _():
        total[...] = jnp.zeros_like(total)
        flipped[...] = normed2_ref[...].T

    @pl.when(jnp.logical_and(step >= 4, step < 8))
    def _():
        unit_sum = jnp.zeros((1, slope_ref.shape[2]), f32)
        for n, (low, high) in enumerate(rows_of(slots, 208)):
            unit = dot(grad_low_ref[low:high, :], down_ref[0], NT) * slope_ref[0, low:high, :].astype(f32)
            unit = unit.astype(bf16)
            grad_unit[low:high, :] = unit
            unit_sum += jnp.sum(unit.astype(f32), axis=0, keepdims=True)
            total[low:high, :] += dot(unit, up_ref[0], NT)
            pump(range(4, 8), n)
        k = step - 4
        for at in range(4):

            @pl.when(k == at)
            def _():
                vectors[0, UNIT_ROW + at:UNIT_ROW + at + 1, :] = unit_sum
        keep_up[k] = dot(flipped[halves_of[0], :], grad_unit[...]).astype(bf16)
        for at in range(4):

            @pl.when(k == at)
            def _():
                down.given(at)
        give_up[k] = dot(flipped[halves_of[1], :], grad_unit[...]).astype(bf16)
        each_send(up, 0, [(k, 4 + k) for k in range(4)])
        pump(range(4, 8), 4)

    @pl.when(step == 7)
    def _():
        gain, attn_scale = gain2_ref[...].astype(f32), attn_scale_ref[...].astype(f32)

        def body(i, sums):
            here = pl.ds(pl.multiple_of(i * 64, 64), 64)
            valid, _, start = start_of(inputs_ref, column_ref, flag_ref, token_ref, here)
            grad_final = valid * grad_out_ref[here, :].astype(f32)
            grad_normed = total[here, :]
            _, scaled, inverse = layer_norm(middle_ref[here, :], gain, gain)
            grad_middle = grad_final + norm_back(grad_normed, scaled, inverse, gain)
            grad_branch1 = attn_scale * grad_middle
            grad_inputs_ref[here, :] = grad_middle
            grad_unit[here, :] = grad_branch1.astype(bf16)
            new = (grad_branch1, (middle_ref[here, :] - start) / attn_scale * grad_middle, grad_normed * scaled, grad_normed)
            return tuple(a + jnp.sum(b, axis=0, keepdims=True) for a, b in zip(sums, new))

        zero = jnp.zeros((1, width), f32)
        sums = lax.fori_loop(0, slots // 64, body, (zero,) * 4)
        for n in range(4):
            vectors[0, 3 + n:4 + n, :] = sums[n]
        total[...] = jnp.zeros_like(total)
        flipped[...] = normed1_ref[...].T

    attending = range(8, 12)
    shard_of = {8: 1, 9: 2, 10: 3, 11: 0}

    @pl.when(jnp.logical_and(step >= 8, step < 12))
    def _():
        k = lax.rem(step - 7, 4)
        grad_low1 = grad_unit
        for low in range(0, slots, 208):
            grad_mixed[low:low + 208, :] = dot(grad_low1[low:low + 208, :], proj_ref[0], NT).astype(bf16)
        value = dot(mixed_ref[0], grad_low1[...], TN).astype(bf16)
        rows = value.shape[0] // 2
        for own in (0, 1):

            @pl.when(core == own)
            def _():
                keep_proj[k] = value[own * rows:(own + 1) * rows]
                give_proj[k] = value[(1 - own) * rows:(2 - own) * rows]
        each_send(proj, 0, [(shard_of[at], at) for at in attending])
        unit = 0
        tiles = windows(slots)
        for head in range(3):
            base = head * triple
            own = slice(head * size, (head + 1) * size)
            for low, high, _, _ in tiles:
                product = grad_mixed[low:high, own].astype(f32) * mixed_ref[0, low:high, own].astype(f32)
                delta[0:1, low:high] = as_row(jnp.sum(product, axis=1, keepdims=True))
            grad_query[...] = jnp.zeros_like(grad_query)
            for low, high, begin, end in tiles:
                keys = packed_ref[0, low:high, base + size:base + 2 * size]
                values = packed_ref[0, low:high, base + 2 * size:base + 3 * size]
                query = packed_ref[0, begin:end, base:base + size] * jnp.bfloat16(scale)
                grads = grad_mixed[begin:end, own]
                scores = dot(keys, query, NT)
                same = column_ref[low:high, :] == row_ref[:, begin:end]
                shares = jnp.exp(jnp.where(same, scores - lse_ref[0, head:head + 1, begin:end], FLOOR_SCORE))
                grad_shares = dot(values, grads, NT)
                grad_scores = (shares * (grad_shares - delta[0:1, begin:end])).astype(bf16)
                grad_packed[low:high, base + 2 * size:base + 3 * size] = dot(shares.astype(bf16), grads).astype(bf16)
                grad_packed[low:high, base + size:base + 2 * size] = dot(grad_scores, query).astype(bf16)
                grad_query[begin:end, :] += dot(grad_scores, keys, TN)
                pump(attending, unit)
                unit += 1
            grad_packed[:, base:base + size] = (grad_query[...] * scale).astype(bf16)
        keep_heads[k] = dot(flipped[halves_of[0], :], grad_packed[...]).astype(bf16)
        give_heads[k] = dot(flipped[halves_of[1], :], grad_packed[...]).astype(bf16)
        each_send(heads, 0, [(shard_of[at], at) for at in attending])
        sums = jnp.sum(grad_packed[...].astype(f32), axis=0, keepdims=True)
        for at in range(4):

            @pl.when(k == at)
            def _():
                vectors[0, HEAD_ROW + at:HEAD_ROW + at + 1, :sums.shape[1]] = sums
        for low in range(0, slots, 208):
            total[low:low + 208, :] += dot(grad_packed[low:low + 208, :], heads_ref[0], NT)
        pump(attending, 21)

    @pl.when(step == 12)
    def _():
        gain = gain1_ref[...].astype(f32)

        def body(i, sums):
            here = pl.ds(pl.multiple_of(i * 64, 64), 64)
            valid, flagged, start = start_of(inputs_ref, column_ref, flag_ref, token_ref, here)
            _, scaled, inverse = layer_norm(start, gain, gain)
            grad_normed = total[here, :]
            grad_start = grad_inputs_ref[here, :] + norm_back(grad_normed, scaled, inverse, gain)
            grad_inputs_ref[here, :] = valid * (1.0 - flagged) * grad_start
            new = (valid * flagged * grad_start, grad_normed * scaled, grad_normed)
            return tuple(a + jnp.sum(b, axis=0, keepdims=True) for a, b in zip(sums, new))

        zero = jnp.zeros((1, width), f32)
        sums = (zero,) * 3
        for n, (low, high) in enumerate(((0, 4), (4, 8), (8, slots // 64))):
            sums = lax.fori_loop(low, high, body, sums)
            pump((12,), n)
        for n in range(3):
            vectors[0, n:n + 1, :] = sums[n]
        vector_copy(0).start()
        pump((12,), 3)
        for action in tail:
            action()
        last_level = len(levels)
        for k in (1, 2, 3):
            vector_copy(last_level + k - 1).wait_recv()
        mine = vectors[last_level]
        vector_ref[...] = mine + vector_tp[0] + vector_tp[1] + vector_tp[2]
        for row_at in (UNIT_ROW, HEAD_ROW):
            value = mine[row_at:row_at + 1]
            for k in (1, 2, 3):
                value += vector_tp[k - 1, row_at + k:row_at + k + 1, :]
            vector_ref[row_at:row_at + 1, :] = value
        for n in range(last_level + 3):
            vector_copy(n).wait_send()
        down.step6(1)
        for item in (up, heads, proj):
            item.step6()


def back(grad_low, hidden, slope, down, up, normed2, middle, grad_out, inputs, normed1, packed, mixed, lse,
         heads, proj, column, row, flag, token, gain1, gain2, attn_scale, sums):
    slots, width = normed2.shape
    units, columns, part = hidden.shape[2], heads.shape[2], mixed.shape[2]
    levels = lax.axis_size("dp").bit_length() - 1
    clip = lambda low, high: lambda at: jnp.minimum(jnp.maximum(at, low), high)
    in_down, in_up = clip(0, 3), lambda at: clip(4, 7)(at) - 4
    in_heads = lambda at: lax.rem(clip(8, 11)(at) - 7, 4)
    once = lambda *shape: pl.BlockSpec(shape, lambda at: (0,) * len(shape), pipeline_mode=pl.Buffered(1))
    tokens, vector, anywhere = once(slots, width), once(1, width), pl.BlockSpec(memory_space=pl.ANY)
    shapes = [(units, width), (width, units), (width, columns), (part, width)]
    got = []
    for n, (rows, cols) in enumerate(shapes):
        eighth = (rows // 4, cols // 2) if n == 3 else (rows // 8, cols)
        got += [pltpu.VMEM((4, rows // 2, cols), bf16), pltpu.VMEM((4, rows // 4, cols), bf16),
                pltpu.VMEM((4,) + eighth, bf16), pltpu.VMEM((3,) + eighth, bf16), pltpu.VMEM(eighth, bf16)]
    half = [pltpu.VMEM((4, rows // 2, cols), bf16) for rows, cols in shapes]
    return pl.pallas_call(
        back_kernel,
        grid=(13,),
        in_specs=[
            tokens, each(slots, units, at=in_down), each(slots, units, at=in_up), each(units, width, at=in_up),
            each(width, units, at=in_up), tokens, tokens, tokens, tokens, tokens,
            each(slots, columns, at=in_heads), each(slots, part, at=in_heads), each(8, slots, at=in_heads),
            each(width, columns, at=in_heads), each(part, width, at=in_heads), once(slots, 1), once(1, slots),
            once(slots, 1), vector, vector, vector, vector, once(8, width),
        ],
        out_specs=[once(slots, width), once(VECTORS, width), anywhere, anywhere, anywhere, anywhere],
        out_shape=[jax.ShapeDtypeStruct((slots, width), f32), jax.ShapeDtypeStruct((VECTORS, width), f32)]
        + [jax.ShapeDtypeStruct(shape, bf16) for shape in shapes],
        scratch_shapes=[
            pltpu.VMEM((slots, units), bf16), pltpu.VMEM((slots, width), f32), pltpu.VMEM((width, slots), bf16),
            pltpu.VMEM((slots, part), bf16), pltpu.VMEM((slots, columns), bf16), pltpu.VMEM((8, slots), f32),
            pltpu.VMEM((slots, columns // 9), f32),
        ] + half + [half[0]] + half[2:] + [
            pltpu.VMEM((levels + 1, VECTORS, width), f32), pltpu.VMEM((levels, VECTORS, width), f32),
            pltpu.VMEM((3, VECTORS, width), f32), pltpu.SemaphoreType.DMA((levels + 3,)),
            pltpu.SemaphoreType.DMA((levels + 3,)), pltpu.SemaphoreType.DMA((4,)),
        ] + got + [pltpu.SemaphoreType.DMA((Reduce.COPIES,))] * 8,
        compiler_params=pltpu.CompilerParams(vmem_limit_bytes=65400 << 10, collective_id=1, has_side_effects=True),
        cost_estimate=cost(36e9, 60e6, 12 * 480000),
        name="back",
    )(grad_low, hidden, slope, down, up, normed2, middle, grad_out, inputs, normed1, packed, mixed, lse,
      heads, proj, column, row, flag, token, gain1, gain2, attn_scale, sums)


def others(value):
    return [exchange(value, 0, k) for k in (1, 2, 3)]


def local(
    inputs,
    segment_ids,
    mask_flags,
    mask_token,
    norm_gain,
    norm_shift,
    heads_weight,
    heads_bias,
    proj_weight,
    proj_bias,
    attn_scale,
    mlp_gain,
    mlp_shift,
    up_weight,
    up_bias,
    down_weight,
    down_bias,
    mlp_scale,
    grad_out,
):
    slots = mask_flags.shape[1]
    own_rows = mask_flags.shape[0]
    width = inputs.shape[1]
    triple = heads_weight.shape[2]
    head_size = triple // 3
    heads_here = heads_weight.shape[1]
    own_ids = lax.dynamic_slice_in_dim(segment_ids, lax.axis_index("tp") * own_rows, own_rows, 0)
    column, row = own_ids.reshape(-1, 1), own_ids.reshape(1, -1)
    flag = mask_flags.reshape(-1, 1)
    vector = lambda v: v.reshape(1, -1)
    token, gain1, gain2 = vector(mask_token), vector(norm_gain), vector(mlp_gain)
    own_heads = heads_weight.reshape(width, -1)
    heads_cols = own_heads.shape[1]

    own_bias = jnp.concatenate([head_bias_row(heads_bias, head_size), up_bias.astype(f32).reshape(1, -1)], axis=1)
    bias = jnp.stack([own_bias] + others(own_bias))
    head_bias, unit_bias = bias[:, :, :heads_cols], bias[:, :, heads_cols:]

    normed1, packed, mixed, lse, heads_all, up_all, proj_all, down_all = gather_attend(
        inputs, column, row, flag, token, gain1, vector(norm_shift), head_bias, own_heads, up_weight, proj_weight,
        down_weight,
    )
    proj_flat = proj_all.reshape(-1, width)
    middle, normed2, hidden, slope, output, grad_low2, sums_a = mlp(
        inputs, column, flag, token, mixed, proj_flat, vector(proj_bias), vector(attn_scale), gain2,
        vector(mlp_shift), up_all, unit_bias, down_all, vector(down_bias), vector(mlp_scale), grad_out,
    )
    grad_inputs, small, sum_down, sum_up, sum_heads, sum_proj = back(
        grad_low2, hidden, slope, down_all, up_all, normed2, middle, grad_out, inputs, normed1, packed, mixed,
        lse, heads_all, proj_all, column, row, flag, token, gain1, gain2, vector(attn_scale), sums_a,
    )
    sum_down, sum_up, sum_proj = (item.astype(f32) for item in (sum_down, sum_up, sum_proj))
    sum_heads = sum_heads.astype(f32).reshape(heads_weight.shape)
    bias_sums = small[HEAD_ROW, :heads_cols].reshape(heads_here, triple)
    sum_heads_bias = jnp.concatenate([bias_sums[:, :head_size], bias_sums[:, 2 * head_size:]], axis=1)
    sum_up_bias = small[UNIT_ROW, :up_bias.shape[0]]
    (sum_token, sum_gain1, sum_shift1, sum_proj_bias, sum_scale1, sum_gain2, sum_shift2,
     sum_down_bias, sum_scale2) = [small[i] for i in range(9)]
    return (
        output,
        grad_inputs,
        sum_token,
        sum_gain1,
        sum_shift1,
        sum_heads,
        sum_heads_bias,
        sum_proj,
        sum_proj_bias,
        sum_scale1,
        sum_gain2,
        sum_shift2,
        sum_up,
        sum_up_bias,
        sum_down,
        sum_down_bias,
        sum_scale2,
    )


def solution(mesh):
    placed = (
        P(("dp", "tp"), None),
        P("dp", None),
        P(("dp", "tp"), None),
        P(),
        P(),
        P(),
        P(None, "tp", None),
        P("tp", None),
        P("tp", None),
        P(),
        P(),
        P(),
        P(),
        P(None, "tp"),
        P("tp"),
        P("tp", None),
        P(),
        P(),
        P(("dp", "tp"), None),
    )
    return jax.shard_map(
        local,
        mesh=mesh,
        in_specs=placed,
        out_specs=(
            P(("dp", "tp"), None),
            P(("dp", "tp"), None),
            P(),
            P(),
            P(),
            P(None, "tp", None),
            P("tp", None),
            P("tp", None),
            P(),
            P(),
            P(),
            P(),
            P(None, "tp"),
            P("tp"),
            P("tp", None),
            P(),
            P(),
        ),
        check_vma=False,
    )
```

profile of v0, /device:TPU:0, one launch (start us, length us, event | category | flops | bytes accessed | tf_op | source)
XLA Modules:
  0.0 286.8 jit_solution(14393045079702304805)
XLA Ops:
  0.7 0.0 copy-start
  0.7 0.0 copy-start.8
  0.7 0.0 copy-start.11
  0.8 0.8 reshape.108
  1.6 0.8 slice_convert_fusion.1
  2.4 0.1 pad.9.clone
  2.5 0.1 reshape.94
  2.6 0.1 pad_maximum_fusion.4
  2.6 5.1 %collective-permute-start.2 = (f32[1,1344]{1,0:T(1,128)S(1)}, f32[1,1344]{1,0:T(1,128)S(1)}, u32[]{:S(2)}, u32[]{:S(2)}) collective-permute-start(f32[1,1344]{1,0:T(1,128)S(1)} %pad_maximum_fusion.4), channel_id=1, source_target_pairs={{0,3},{1,2},{2,1},{3,0},{4,7},{5,6},{6,5},{7,4},{8,11},{9,10},{10,... | collective-permute-start | bytes 16136 | tf_op jit(solution)/shard_map/ppermute | solution.py:62
  7.7 0.0 collective-permute-start.1
  7.7 0.6 collective-permute-start
  8.3 0.1 fusion.1
  8.5 0.0 copy-start.3
  8.5 0.2 copy.41.column_ref
  8.7 0.0 copy-start.1
  8.7 0.9 copy.42.flag_ref
  9.6 0.0 copy-start.2
  9.6 0.7 reshape.91.token_ref
  10.3 0.7 reshape.92.gain_ref.gain1_ref
  11.0 0.7 reshape.93.shift_ref
  11.7 1.5 copy.40.heads_ref
  13.2 0.0 copy-done.24
  13.2 0.0 copy-done.25
  13.3 0.0 copy-start.6
  13.3 0.0 copy-done.27
  13.3 0.0 copy-start.7
  13.3 0.0 copy-done.28
  13.4 0.0 copy-done.29
  13.4 0.0 collective-permute-done.2
  13.4 0.0 collective-permute-done.1
  13.4 0.0 collective-permute-done
  13.4 0.1 pad_maximum_fusion.unit_bias_ref
  13.5 0.0 copy-start.9
  13.6 1.3 copy-done.9
  14.8 1.3 copy-done.10
  16.1 70.2 %gather_attend.1 = (bf16[832,768]{1,0:T(8,128)(2,1)S(1)}, bf16[4,832,576]{2,1,0:T(8,128)(2,1)}, bf16[4,832,192]{2,1,0:T(8,128)(2,1)S(1)}, f32[4,8,832]{2,1,0:T(8...) custom-call(bf16[832,768]{1,0:T(8,128)(2,1)S(1)} %copy-done.8, ...), custom_call_target="tpu_custom_call" | custom-call | flops 16000000000 | bytes 40000000 | tf_op jit(solution)/shard_map/gather_attend/pallas_call | solution.py:316
  86.3 0.0 copy-done.3
  86.3 0.0 copy-done.5
  86.3 0.0 copy-start.13
  86.3 1.2 copy-done.13
  87.5 2.0 copy-done.16
  89.5 1.1 copy-done.17
  90.6 0.6 copy-done.19
  91.2 0.0 copy-done.4
  91.2 0.0 copy-done.6
  91.2 0.0 copy-done.7
  91.3 22.0 %mlp.1 = (f32[832,768]{1,0:T(8,128)}, bf16[832,768]{1,0:T(8,128)(2,1)S(1)}, bf16[4,832,768]{2,1,0:T(8,128)(2,1)}, bf16[4,832,768]{2,1,0:T(8,128)(2,1)}, bf16[832...) custom-call(bf16[832,768]{1,0:T(8,128)(2,1)S(1)} %copy-done.8, ...), custom_call_target="tpu_custom_call" | custom-call | flops 8999999488 | bytes 30000000 | tf_op jit(solution)/shard_map/mlp/pallas_call | solution.py:398
  113.3 0.0 copy-start.14
  113.3 1.0 copy-done.14
  114.3 1.0 copy-done.15
  115.3 0.6 copy-done.18
  116.0 159.0 %back.1 = (f32[832,768]{1,0:T(8,128)}, f32[24,768]{1,0:T(8,128)}, bf16[768,768]{1,0:T(8,128)(2,1)}, bf16[768,768]{1,0:T(8,128)(2,1)}, bf16[768,576]{1,0:T(8,128)(2,1)}, /*index=5*/bf16[192,768]{1,0:T(8,128)(2,1)}) custom-call(bf16[832,768]{1,0:T(8,128)(2,1)} %copy-done.15, bf16[4,832,768]{2,1,0:T(8,128)(2,1)} %get-tuple-element.44.hidden_ref, ...), custom_call_target="tpu_custom_call" | custom-call | flops 35999997952 | bytes 60000000 | tf_op jit(solution)/shard_map/back/pallas_call | solution.py:841
  275.0 1.7 slice_reduce_fusion
  276.7 0.7 slice_reduce_fusion.10
  277.5 0.0 copy-start.22
  277.5 2.5 copy.45
  280.0 0.1 reshape_squeeze.3
  280.1 0.9 convert_element_type.19
  280.9 1.6 convert_element_type.20
  282.5 0.1 copy-done.21
  282.6 1.6 convert_element_type.21
  284.2 0.7 pad_maximum_fusion.6
  284.8 0.3 copy-done.20
  285.2 1.5 copy.47
  (39 shorter events, 0.1 us)
Async XLA Ops:
  0.7 7.8 %copy-start = (s32[4,832]{1,0:T(4,128)S(1)}, s32[4,832]{1,0:T(4,128)}, u32[]{:S(2)}) copy-start(s32[4,832]{1,0:T(4,128)} %param.20) | copy-start | bytes 39940
  0.7 12.5 %copy-start.24 = (bf16[768]{0:T(1024)(128)(2,1)S(1)}, bf16[768]{0:T(1024)(128)(2,1)}, u32[]{:S(2)}) copy-start(bf16[768]{0:T(1024)(128)(2,1)} %param.28) | copy-start | bytes 4612
  0.7 12.6 %copy-start.25 = (bf16[768]{0:T(1024)(128)(2,1)S(1)}, bf16[768]{0:T(1024)(128)(2,1)}, u32[]{:S(2)}) copy-start(bf16[768]{0:T(1024)(128)(2,1)} %param.29) | copy-start | bytes 4612
  0.7 12.6 %copy-start.26 = (bf16[768]{0:T(1024)(128)(2,1)S(1)}, bf16[768]{0:T(1024)(128)(2,1)}, u32[]{:S(2)}) copy-start(bf16[768]{0:T(1024)(128)(2,1)} %param.30) | copy-start | bytes 4612
  0.7 12.6 %copy-start.27 = (bf16[768]{0:T(1024)(128)(2,1)S(1)}, bf16[768]{0:T(1024)(128)(2,1)}, u32[]{:S(2)}) copy-start(bf16[768]{0:T(1024)(128)(2,1)} %param.31) | copy-start | bytes 4612
  0.7 12.6 %copy-start.28 = (bf16[768]{0:T(1024)(128)(2,1)S(1)}, bf16[768]{0:T(1024)(128)(2,1)}, u32[]{:S(2)}) copy-start(bf16[768]{0:T(1024)(128)(2,1)} %param.35) | copy-start | bytes 4612
  0.7 12.6 %copy-start.29 = (bf16[768]{0:T(1024)(128)(2,1)S(1)}, bf16[768]{0:T(1024)(128)(2,1)}, u32[]{:S(2)}) copy-start(bf16[768]{0:T(1024)(128)(2,1)} %param.36) | copy-start | bytes 4612
  0.7 12.8 %copy-start.8 = (bf16[832,768]{1,0:T(8,128)(2,1)S(1)}, bf16[832,768]{1,0:T(8,128)(2,1)}, u32[]{:S(2)}) copy-start(bf16[832,768]{1,0:T(8,128)(2,1)} %inputs_ref.5) | copy-start | bytes 3833860
  0.7 12.8 %copy-start.11 = (bf16[192,768]{1,0:T(8,128)(2,1)S(1)}, bf16[192,768]{1,0:T(8,128)(2,1)}, u32[]{:S(2)}) copy-start(bf16[192,768]{1,0:T(8,128)(2,1)} %proj_ref.1) | copy-start | bytes 884740
  2.6 10.7 %collective-permute-start.2 = (f32[1,1344]{1,0:T(1,128)S(1)}, f32[1,1344]{1,0:T(1,128)S(1)}, u32[]{:S(2)}, u32[]{:S(2)}) collective-permute-start(f32[1,1344]{1,0:T(1,128)S(1)} %pad_maximum_fusion.4), channel_id=1, source_target_pairs={{0,3},{1,2},{2,1},{3,0},{4,7},{5,6},{6,5},{7,4},{8,11},{9,10},{10,... | collective-permute-start | bytes 16136 | tf_op jit(solution)/shard_map/ppermute | solution.py:62
  7.7 5.7 %collective-permute-start.1 = (f32[1,1344]{1,0:T(1,128)S(1)}, f32[1,1344]{1,0:T(1,128)S(1)}, u32[]{:S(2)}, u32[]{:S(2)}) collective-permute-start(f32[1,1344]{1,0:T(1,128)S(1)} %pad_maximum_fusion.4), channel_id=1, source_target_pairs={{0,2},{1,3},{2,0},{3,1},{4,6},{5,7},{6,4},{7,5},{8,10},{9,11},{10,... | collective-permute-start | bytes 16136 | tf_op jit(solution)/shard_map/ppermute | solution.py:62
  7.7 5.7 %collective-permute-start = (f32[1,1344]{1,0:T(1,128)S(1)}, f32[1,1344]{1,0:T(1,128)S(1)}, u32[]{:S(2)}, u32[]{:S(2)}) collective-permute-start(f32[1,1344]{1,0:T(1,128)S(1)} %pad_maximum_fusion.4), channel_id=1, source_target_pairs={{0,1},{1,0},{2,3},{3,2},{4,5},{5,4},{6,7},{7,6},{8,9},{9,8},{10,11... | collective-permute-start | bytes 16136 | tf_op jit(solution)/shard_map/ppermute | solution.py:62
  8.5 77.9 %copy-start.3 = (s32[1,832]{1,0:T(1,128)}, s32[1,832]{1,0:T(1,128)S(1)}, u32[]{:S(2)}) copy-start(s32[1,832]{1,0:T(1,128)S(1)} %constant_dynamic-slice_fusion.row_ref) | copy-start | bytes 9988
  8.7 82.6 %copy-start.1 = (s32[832,1]{1,0:T(8,128)}, s32[832,1]{1,0:T(8,128)S(1)}, u32[]{:S(2)}) copy-start(s32[832,1]{1,0:T(8,128)S(1)} %copy.41.column_ref) | copy-start | bytes 9988
  9.6 81.7 %copy-start.2 = (s32[832,1]{1,0:T(8,128)}, s32[832,1]{1,0:T(8,128)S(1)}, u32[]{:S(2)}) copy-start(s32[832,1]{1,0:T(8,128)S(1)} %copy.42.flag_ref) | copy-start | bytes 9988
  10.3 80.9 %copy-start.4 = (bf16[1,768]{1,0:T(2,128)(2,1)}, bf16[1,768]{1,0:T(2,128)(2,1)S(1)}, u32[]{:S(2)}) copy-start(bf16[1,768]{1,0:T(2,128)(2,1)S(1)} %reshape.91.token_ref) | copy-start | bytes 4612
  11.0 75.3 %copy-start.5 = (bf16[1,768]{1,0:T(2,128)(2,1)}, bf16[1,768]{1,0:T(2,128)(2,1)S(1)}, u32[]{:S(2)}) copy-start(bf16[1,768]{1,0:T(2,128)(2,1)S(1)} %reshape.92.gain_ref.gain1_ref) | copy-start | bytes 4612
  13.3 78.0 %copy-start.6 = (bf16[1,768]{1,0:T(2,128)(2,1)}, bf16[1,768]{1,0:T(2,128)(2,1)S(1)}, u32[]{:S(2)}) copy-start(bf16[1,768]{1,0:T(2,128)(2,1)S(1)} %reshape.100.attn_scale_ref) | copy-start | bytes 4612
  13.3 77.9 %copy-start.7 = (bf16[1,768]{1,0:T(2,128)(2,1)}, bf16[1,768]{1,0:T(2,128)(2,1)S(1)}, u32[]{:S(2)}) copy-start(bf16[1,768]{1,0:T(2,128)(2,1)S(1)} %reshape.101.gain_ref.gain2_ref) | copy-start | bytes 4612
  13.5 1.3 copy-start.9
  14.8 1.3 copy-start.10
  86.3 1.2 copy-start.13
  87.5 2.0 copy-start.16
  89.5 1.1 copy-start.17
  90.6 0.6 copy-start.19
  91.2 22.0 %copy-start.12 = (bf16[4,192,768]{2,1,0:T(8,128)(2,1)}, bf16[4,192,768]{2,1,0:T(8,128)(2,1)S(1)}, u32[]{:S(2)}) copy-start(bf16[4,192,768]{2,1,0:T(8,128)(2,1)S(1)} %get-tuple-element.39.proj_ref) | copy-start | bytes 3538948
  113.3 1.0 copy-start.14
  114.3 1.0 copy-start.15
  115.3 0.6 copy-start.18
  275.0 5.1 %copy-start.23 = (bf16[192,768]{1,0:T(8,128)(2,1)S(1)}, bf16[192,768]{1,0:T(8,128)(2,1)}, u32[]{:S(2)}) copy-start(bf16[192,768]{1,0:T(8,128)(2,1)} %get-tuple-element.56) | copy-start | bytes 884740
  277.5 3.5 %copy-start.22 = (bf16[768,768]{1,0:T(8,128)(2,1)S(1)}, bf16[768,768]{1,0:T(8,128)(2,1)}, u32[]{:S(2)}) copy-start(bf16[768,768]{1,0:T(8,128)(2,1)} %get-tuple-element.57) | copy-start | bytes 3538948
  280.9 1.7 copy-start.21
  282.6 2.6 copy-start.20
where the time goes:
time: 289 us; the launch traced here: 287 us
  Pallas kernels  251 us (87%)
  local copies, waits for them, and re-layouts  22.9 us (8%)
  other arithmetic  5.74 us (2%)
  starting transfers between devices  5.7 us (2%)
    pallas_call x1, Pallas kernels, back(): pl.pallas_call(back_kernel, grid=(13,), in_specs=[tokens, each(slots, uni...  159 us
    pallas_call x1, Pallas kernels, gather_attend(): pl.pallas_call(gather_attend_kernel, grid=(4,), in_specs=[whole(slots, wi...  70.2 us
    pallas_call x1, Pallas kernels, mlp(): pl.pallas_call(mlp_kernel, grid=(count,), in_specs=[tokens, whole(slots,...  22 us
    unnamed x61, local copies, waits for them, and re-layouts  12.1 us
  transfers between devices with their start and end apart: 3, of which 0 were waited for; matrix products, arithmetic and copies ran while one was open for 2% of the time, Pallas kernels for 0%

commit v1 on v0

v1 whole, which is shorter than its diff:
```python
import functools

import jax
import jax.numpy as jnp
from jax import lax
from jax.experimental import pallas as pl
from jax.experimental.pallas import tpu as pltpu
from jax.sharding import PartitionSpec as P

EPSILON = 1e-06
FLOOR_SCORE = -1e30
SQRT_HALF = 0.7071067811865476
INV_ROOT_TWO_PI = 0.3989422804014327
LONGEST = 14 * 14 + 1
FIFTH_FROM = 4 * (11 * 11 + 1)
TILE = 128
CORE, X, Y = 1, 2, 4

f32, bf16 = jnp.float32, jnp.bfloat16
NN = (((1,), (0,)), ((), ()))
NT = (((1,), (1,)), ((), ()))
TN = (((0,), (0,)), ((), ()))


def dot(a, b, dims=NN):
    return lax.dot_general(a, b, dims, preferred_element_type=f32)


def layer_norm(values, gain, shift):
    centre = values - jnp.mean(values, axis=-1, keepdims=True)
    inverse = lax.rsqrt(jnp.mean(centre * centre, axis=-1, keepdims=True) + EPSILON)
    scaled = centre * inverse
    return (scaled * gain + shift, scaled, inverse)


def norm_back(grad_normed, scaled, inverse, gain):
    grad_scaled = grad_normed * gain
    first = jnp.mean(grad_scaled, axis=-1, keepdims=True)
    second = jnp.mean(grad_scaled * scaled, axis=-1, keepdims=True)
    return inverse * (grad_scaled - first - scaled * second)


def gelu_parts(inner):
    normal_cdf = 0.5 * (1.0 + lax.erf(inner * SQRT_HALF))
    density = jnp.exp(-0.5 * inner * inner) * INV_ROOT_TWO_PI
    return (inner * normal_cdf, normal_cdf + inner * density)


def windows(slots):
    out = []
    for low in range(0, slots, TILE):
        high = min(low + TILE, slots)
        begin = low - LONGEST + 1
        if low >= FIFTH_FROM:
            begin = min(begin, FIFTH_FROM)
        end = high + LONGEST - 1
        if high > FIFTH_FROM:
            end = slots
        begin = max(begin, 0) // 128 * 128
        end = min((end + 127) // 128 * 128, slots)
        out.append((low, high, begin, end))
    return out


def as_row(column):
    rows = column.shape[0]
    shape = (rows, rows)
    here = lax.broadcasted_iota(jnp.int32, shape, 0) == lax.broadcasted_iota(jnp.int32, shape, 1)
    return jnp.sum(jnp.where(here, column, 0.0), axis=0, keepdims=True)


def whole(*shape):
    return pl.BlockSpec(shape, lambda k: (0,) * len(shape))


def each(*shape, at=lambda k: k):
    return pl.BlockSpec((1,) + shape, lambda k: (at(k),) + (0,) * len(shape))


def params(megabytes):
    return pltpu.CompilerParams(vmem_limit_bytes=megabytes << 20)


def cost(flops, moved, exps=0):
    return pl.CostEstimate(flops=int(flops), transcendentals=int(exps), bytes_accessed=int(moved))


def start_of(inputs_ref, column_ref, flag_ref, token, here):
    valid = (column_ref[here, :] >= 0).astype(f32)
    flagged = (flag_ref[here, :] == 1).astype(f32)
    start = valid * (flagged * token + (1.0 - flagged) * inputs_ref[here, :].astype(f32))
    return valid, flagged, start


def blocks(columns, step=256):
    return [slice(low, min(low + step, columns)) for low in range(0, columns, step)]


def rows_of(slots, step=104):
    return [(low, min(low + step, slots)) for low in range(0, slots, step)]


def flip(index, bits):
    bit = 1
    while bit <= bits:
        if bits & bit:
            index = index + bit * (1 - 2 * lax.rem(lax.div(index, bit), 2))
        bit *= 2
    return index


class Gather:
    ROUTES = ("z", "x", "y", "fx", "fy", "c0", "c2", "c4", "c6")
    COPIES = 3 * len(ROUTES)

    def __init__(self, full_ref, by_columns, send_sems, recv_sems):
        self.dp, self.tp = lax.axis_index("dp"), lax.axis_index("tp")
        self.own = lax.rem(self.dp, 8)
        self.full, self.by_columns = full_ref, by_columns
        self.sends, self.recvs = send_sems, recv_sems
        _, rows, columns = full_ref.shape
        self.rows, self.columns = (rows // 4, columns // 2) if by_columns else (rows // 8, columns)
        self.half = self.rows // 32 * 16

    def piece(self, k, bits, half=None):
        place, columns = flip(self.own, bits), slice(None)
        if self.by_columns:
            columns = pl.ds(pl.multiple_of(lax.rem(place, 2) * self.columns, 128), self.columns)
            place = lax.div(place, 2)
        begin, height = place * self.rows, self.rows
        if half == 0:
            height = self.half
        elif half == 1:
            begin, height = begin + self.half, self.rows - self.half
        return self.full.at[k, pl.ds(pl.multiple_of(begin, 16), height), columns]

    def copy(self, k, route):
        if route == "z":
            source, target, to = self.piece(0, 0), self.piece(k, 0), (self.dp, flip(self.tp, k))
        else:
            bits, half, link = {
                "x": (0, None, X), "y": (0, None, Y), "fx": (Y, 1, X), "fy": (X, 0, Y),
                "c0": (0, None, CORE), "c2": (X, None, CORE), "c4": (Y, None, CORE), "c6": (X | Y, None, CORE),
            }[route]
            source = target = self.piece(k, bits, half)
            to = (flip(self.dp, link), self.tp)
        n = (k - 1) * len(self.ROUTES) + self.ROUTES.index(route)
        return pltpu.make_async_remote_copy(
            src_ref=source, dst_ref=target, send_sem=self.sends.at[n], recv_sem=self.recvs.at[n],
            device_id=to, device_id_type=pl.DeviceIdType.MESH,
        )

    def start(self, k, *routes):
        for route in routes:
            self.copy(k, route).start()

    def arrived(self, k, *routes):
        for route in routes:
            self.copy(k, route).wait_recv()

    def begin(self, k):
        self.start(k, "z")

    def step1(self, k):
        self.arrived(k, "z")
        self.start(k, "x", "y", "c0")

    def step2(self, k):
        self.arrived(k, "x")
        self.start(k, "fy", "c2")
        self.arrived(k, "y")
        self.start(k, "fx", "c4")

    def step3(self, k):
        self.arrived(k, "fx", "fy")
        self.start(k, "c6")

    def step4(self, k):
        self.arrived(k, "c0", "c2", "c4", "c6")

    def sent(self):
        for k in (1, 2, 3):
            for route in self.ROUTES:
                self.copy(k, route).wait_send()


def meet(peers):
    barrier = pltpu.get_barrier_semaphore()
    for peer in peers:
        pl.semaphore_signal(barrier, inc=1, device_id=peer, device_id_type=pl.DeviceIdType.MESH)
    pl.semaphore_wait(barrier, len(peers))


def as_column(row):
    size = row.shape[1]
    shape = (size, size)
    here = lax.broadcasted_iota(jnp.int32, shape, 0) == lax.broadcasted_iota(jnp.int32, shape, 1)
    return jnp.sum(jnp.where(here, row, 0), axis=1, keepdims=True)


def dispatch(table, step, steps, unit):
    for at in steps:
        if table.get((at, unit)):

            @pl.when(step == at)
            def _():
                for action in table[(at, unit)]:
                    action()


TOKEN, GAIN1, SHIFT1, PROJ_BIAS, ATTN_SCALE, GAIN2, SHIFT2, DOWN_BIAS, MLP_SCALE = range(9)

HEADS, UP, PROJ, DOWN = range(4)
FORWARD_PLAN = {
    (0, 1): ((HEADS, (1, 2), 1),),
    (0, 6): ((HEADS, (3,), 1), (HEADS, (1,), 2),),
    (1, -1): ((PROJ, (1, 2, 3), 0), (UP, (1, 2, 3), 0), (HEADS, (2, 3), 2), (PROJ, (1,), 1), (HEADS, (1, 2), 3), (PROJ, (2, 3), 1), (HEADS, (3,), 3), (HEADS, (1,), 4),),
    (1, 1): ((HEADS, (2,), 4), (PROJ, (1, 2), 2), (UP, (1,), 1),),
    (1, 3): ((HEADS, (3,), 4), (PROJ, (3,), 2),),
    (1, 6): ((DOWN, (1, 2, 3), 0), (UP, (2,), 1), (PROJ, (1, 2), 3),),
    (2, 1): ((UP, (1,), 2), (PROJ, (3,), 3), (UP, (3,), 1), (PROJ, (1, 2), 4),),
    (2, 3): ((DOWN, (1,), 1),),
    (2, 6): ((UP, (2,), 2), (PROJ, (3,), 4), (UP, (1,), 3),),
    (3, 1): ((DOWN, (2,), 1), (UP, (3,), 2),),
    (3, 3): ((UP, (1,), 4),),
    (3, 6): ((DOWN, (1,), 2), (DOWN, (3,), 1), (UP, (2,), 3),),
    (4, 1): ((UP, (2,), 4), (UP, (3,), 3), (DOWN, (2,), 2),),
    (4, 3): ((DOWN, (1,), 3),),
    (5, -1): ((DOWN, (3,), 2), (UP, (3,), 4), (DOWN, (2,), 3), (DOWN, (1,), 4),),
    (5, 3): ((DOWN, (3,), 3), (DOWN, (2,), 4),),
    (6, 3): ((DOWN, (3,), 4),),
}


def forward_kernel(
    inputs_ref, segment_ref, mask_ref, vectors_ref, heads_bias_ref, unit_bias_ref, grad_out_ref,
    heads_ref, up_ref, proj_ref, down_ref,
    normed1_ref, column_ref, flag_ref, row_ref, packed_ref, mixed_ref, lse_ref, middle_ref, normed2_ref, hidden_ref,
    slope_ref, output_ref, grad_low_ref, sums_ref, heads_all, up_all, proj_all, down_all,
    heads_now, up_now, proj_now, down_now, head_bias, unit_bias, mixed_all, total,
    own_sems, store_sems, bias_sends, bias_recvs,
    *sems,
):
    slots = inputs_ref.shape[0]
    triple = heads_now.shape[2] // 3
    size = triple // 3
    scale = size ** (-0.5)
    part = mixed_ref.shape[2]
    step = pl.program_id(0)
    vector = lambda n: vectors_ref[n:n + 1, :]
    shards, fulls = (heads_ref, up_ref, proj_ref, down_ref), (heads_all, up_all, proj_all, down_all)
    nows = (heads_now, up_now, proj_now, down_now)
    gathers = [Gather(nows[n], n == PROJ, sems[2 * n], sems[2 * n + 1]) for n in range(4)]
    dp, tp = gathers[0].dp, gathers[0].tp
    loads = [pltpu.make_async_copy(shards[n], nows[n].at[0], own_sems.at[n]) for n in range(4)]
    store = lambda n, k: pltpu.make_async_copy(nows[n].at[k], fulls[n].at[k], store_sems.at[n, k])

    def bias_copy(n, k):
        item = (head_bias, unit_bias)[n]
        return pltpu.make_async_remote_copy(
            src_ref=item.at[0], dst_ref=item.at[k], send_sem=bias_sends.at[n, k], recv_sem=bias_recvs.at[n, k],
            device_id=(dp, flip(tp, k)), device_id_type=pl.DeviceIdType.MESH,
        )

    table = {}
    for key, entries in FORWARD_PLAN.items():
        table[key] = []
        for n, ks, action in entries:
            item = gathers[n]
            for k in ks:
                table[key].append(functools.partial(
                    (item.begin, item.step1, item.step2, item.step3, item.step4)[action], k))
                if action == 4:
                    table[key].append(store(n, k).start)

    @pl.when(step == 0)
    def _():
        for load in loads:
            load.start()
        meet([(dp, flip(tp, k)) for k in (1, 2, 3)] + [(flip(dp, bit), tp) for bit in (X, Y, CORE)])
        loads[HEADS].wait()
        for k in (1, 2, 3):
            gathers[HEADS].begin(k)
        blank = jnp.zeros((1, size), f32)
        pieces = []
        for head in range(3):
            here = heads_bias_ref[head:head + 1, :].astype(f32)
            pieces += [here[:, :size], blank, here[:, size:]]
        head_bias[0] = jnp.broadcast_to(jnp.concatenate(pieces, axis=1), head_bias.shape[1:])
        unit_bias[0] = jnp.broadcast_to(unit_bias_ref[...].astype(f32), unit_bias.shape[1:])
        for n in range(2):
            for k in (1, 2, 3):
                bias_copy(n, k).start()
        row_ref[...] = segment_ref[pl.ds(tp, 1), :]
        for low in range(0, slots, 128):
            high = min(low + 128, slots)
            column_ref[low:high, :] = as_column(row_ref[:, low:high])
            flag_ref[low:high, :] = as_column(mask_ref[:, low:high])

        def body(i, carry):
            here = pl.ds(pl.multiple_of(i * 64, 64), 64)
            _, _, start = start_of(inputs_ref, column_ref, flag_ref, vector(TOKEN), here)
            normed1_ref[here, :] = layer_norm(start, vector(GAIN1), vector(SHIFT1))[0].astype(bf16)
            return carry

        lax.fori_loop(0, slots // 64, body, 0)
        for load in loads[1:]:
            load.wait()
        for n in range(4):
            store(n, 0).start()

    @pl.when(step == 1)
    def _():
        for k in (1, 2, 3):
            bias_copy(0, k).wait_recv()

    dispatch(table, step, range(1, 8), -1)

    @pl.when(step < 4)
    def _():
        for low in range(0, slots, 208):
            product = dot(normed1_ref[low:low + 208, :], heads_now[step])
            packed_ref[0, low:low + 208, :] = (product + head_bias[step, 0:1, :]).astype(bf16)
        lse_ref[...] = jnp.zeros_like(lse_ref)
        bases = [head * triple for head in range(3)]
        for unit, (low, high, begin, end) in enumerate(windows(slots)):
            same = column_ref[low:high, :] == row_ref[:, begin:end]
            scores = [
                dot(packed_ref[0, low:high, base:base + size] * jnp.bfloat16(scale),
                    packed_ref[0, begin:end, base + size:base + 2 * size], NT)
                for base in bases
            ]
            scores = [jnp.where(same, item, FLOOR_SCORE) for item in scores]
            largest = [jnp.max(item, axis=1, keepdims=True) for item in scores]
            raised = [jnp.exp(item - top) for item, top in zip(scores, largest)]
            totals = [jnp.sum(item, axis=1, keepdims=True) for item in raised]
            mixed = [
                dot(item.astype(bf16), packed_ref[0, begin:end, base + 2 * size:base + 3 * size])
                for item, base in zip(raised, bases)
            ]
            mixed = [(item * (1.0 / total)).astype(bf16) for item, total in zip(mixed, totals)]
            mixed_ref[0, low:high, :] = jnp.concatenate(mixed, axis=1)
            for head in range(3):
                lse_ref[0, head:head + 1, low:high] = as_row(largest[head] + jnp.log(totals[head]))
            dispatch(table, step, range(4), unit)

    for k in range(4):

        @pl.when(step == k)
        def _():
            mixed_all[:, k * part:(k + 1) * part] = mixed_ref[0]

    @pl.when(step == 4)
    def _():
        for k in (1, 2, 3):
            bias_copy(1, k).wait_recv()
        total[...] = jnp.zeros_like(total)
        proj = proj_now[...].reshape(-1, proj_now.shape[2])
        for low, high in rows_of(slots, 208):
            middle_ref[low:high, :] = dot(mixed_all[low:high, :], proj) + vector(PROJ_BIAS)

        def body(i, carry):
            here = pl.ds(pl.multiple_of(i * 64, 64), 64)
            _, _, start = start_of(inputs_ref, column_ref, flag_ref, vector(TOKEN), here)
            middle = start + vector(ATTN_SCALE) * middle_ref[here, :]
            middle_ref[here, :] = middle
            normed2_ref[here, :] = layer_norm(middle, vector(GAIN2), vector(SHIFT2))[0].astype(bf16)
            return carry

        lax.fori_loop(0, slots // 64, body, 0)

    @pl.when(step >= 4)
    def _():
        k = step - 4
        for unit, (low, high) in enumerate(rows_of(slots, 208)):
            for columns in blocks(hidden_ref.shape[2]):
                inner = dot(normed2_ref[low:high, :], up_now[k, :, columns]) + unit_bias[k, 0:1, columns]
                value, slope = gelu_parts(inner)
                hidden_ref[0, low:high, columns] = value.astype(bf16)
                slope_ref[0, low:high, columns] = slope.astype(bf16)
            total[low:high, :] += dot(hidden_ref[0, low:high, :], down_now[k])
            dispatch(table, step, range(4, 8), unit)

    @pl.when(step == 7)
    def _():
        def body(i, sums):
            here = pl.ds(pl.multiple_of(i * 64, 64), 64)
            valid = (column_ref[here, :] >= 0).astype(f32)
            branch2 = total[here, :] + vector(DOWN_BIAS)
            output_ref[here, :] = (valid * (middle_ref[here, :] + vector(MLP_SCALE) * branch2)).astype(bf16)
            grad_final = valid * grad_out_ref[here, :].astype(f32)
            grad_branch2 = vector(MLP_SCALE) * grad_final
            grad_low_ref[here, :] = grad_branch2.astype(bf16)
            return tuple(a + jnp.sum(b, axis=0, keepdims=True) for a, b in zip(sums, (branch2 * grad_final, grad_branch2)))

        zero = jnp.zeros((1, inputs_ref.shape[1]), f32)
        sums = lax.fori_loop(0, slots // 64, body, (zero, zero))
        sums_ref[...] = jnp.zeros_like(sums_ref)
        sums_ref[0:1, :], sums_ref[1:2, :] = sums
        for n, item in enumerate(gathers):
            item.sent()
            for k in range(4):
                store(n, k).wait()
        for n in range(2):
            for k in (1, 2, 3):
                bias_copy(n, k).wait_send()


def once(*shape):
    return pl.BlockSpec(shape, lambda at: (0,) * len(shape), pipeline_mode=pl.Buffered(1))


def forward(inputs, segments, mask, vectors, heads_bias, unit_bias, grad_out, heads, up, proj, down):
    slots, width = inputs.shape
    columns, units = heads.shape[1], up.shape[1]
    part = columns // 3
    anywhere = pl.BlockSpec(memory_space=pl.ANY)
    early = lambda at: jnp.minimum(at, 3)
    late = lambda at: jnp.maximum(at - 4, 0)
    tokens = once(slots, width)
    shape = jax.ShapeDtypeStruct
    return pl.pallas_call(
        forward_kernel,
        grid=(8,),
        in_specs=[
            tokens, once(*segments.shape), once(1, slots), once(*vectors.shape), once(*heads_bias.shape),
            once(*unit_bias.shape), tokens, anywhere, anywhere, anywhere, anywhere,
        ],
        out_specs=[
            tokens, once(slots, 1), once(slots, 1), once(1, slots), each(slots, columns, at=early),
            each(slots, part, at=early), each(8, slots, at=early), tokens, tokens, each(slots, units, at=late),
            each(slots, units, at=late), tokens, tokens, once(8, width), anywhere, anywhere, anywhere, anywhere,
        ],
        out_shape=[
            shape((slots, width), bf16), shape((slots, 1), jnp.int32), shape((slots, 1), jnp.int32),
            shape((1, slots), jnp.int32), shape((4, slots, columns), bf16), shape((4, slots, part), bf16),
            shape((4, 8, slots), f32), shape((slots, width), f32), shape((slots, width), bf16),
            shape((4, slots, units), bf16), shape((4, slots, units), bf16), shape((slots, width), bf16),
            shape((slots, width), bf16), shape((8, width), f32),
        ] + [shape((4,) + item.shape, bf16) for item in (heads, up, proj, down)],
        scratch_shapes=[
            pltpu.VMEM((4,) + heads.shape, bf16), pltpu.VMEM((4,) + up.shape, bf16), pltpu.VMEM((4,) + proj.shape, bf16),
            pltpu.VMEM((4,) + down.shape, bf16), pltpu.VMEM((4, 8, columns), f32), pltpu.VMEM((4, 8, units), f32),
            pltpu.VMEM((slots, width), bf16), pltpu.VMEM((slots, width), f32),
            pltpu.SemaphoreType.DMA((4,)), pltpu.SemaphoreType.DMA((4, 4)), pltpu.SemaphoreType.DMA((2, 4)), pltpu.SemaphoreType.DMA((2, 4)),
        ] + [pltpu.SemaphoreType.DMA((Gather.COPIES,))] * 8,
        compiler_params=pltpu.CompilerParams(vmem_limit_bytes=60 << 20, collective_id=0, has_side_effects=True),
        cost_estimate=cost(26e9, 60e6, 6e6),
        name="forward",
    )(inputs, segments, mask, vectors, heads_bias, unit_bias, grad_out, heads, up, proj, down)


class Reduce:
    COPIES = 4 * 4 + 7

    def __init__(self, first, second, by_columns, keep, give, got, out, send_sems, recv_sems, own_sem):
        self.dp, self.tp = lax.axis_index("dp"), lax.axis_index("tp")
        self.first, self.second, self.by_columns = first, second, by_columns
        self.keep, self.give, self.out = keep, give, out
        self.got0, self.got1, self.got2, self.got_tp, self.total = got
        self.sends, self.recvs, self.own_sem = send_sems, recv_sems, own_sem
        self.rows, self.columns = keep.shape[1] * 2, keep.shape[2]
        self.bits = tuple(lax.rem(lax.div(self.dp, bit), 2) for bit in (CORE, first, second))

    def quarter(self, first):
        rows = self.rows // 4
        return pl.multiple_of(first * rows, 16), rows

    def eighth(self, first, second):
        begin, rows = self.quarter(first)
        if self.by_columns:
            width = self.columns // 2
            return begin, rows, pl.ds(pl.multiple_of(second * width, 128), width)
        return pl.multiple_of(begin + second * (rows // 2), 16), rows // 2, slice(None)

    def part(self, ref, spot):
        begin, rows, columns = spot
        return ref.at[pl.ds(begin, rows), columns]

    def place(self, flips):
        core, first, second = (1 - bit if turned else bit for bit, turned in zip(self.bits, flips))
        begin, rows, columns = self.eighth(first, second)
        return self.out.at[pl.ds(pl.multiple_of(core * (self.rows // 2) + begin, 16), rows), columns]

    def remote(self, n, source, target, bits=0, k=0):
        return pltpu.make_async_remote_copy(
            src_ref=source, dst_ref=target, send_sem=self.sends.at[n], recv_sem=self.recvs.at[n],
            device_id=(flip(self.dp, bits), flip(self.tp, k)), device_id_type=pl.DeviceIdType.MESH,
        )

    def copy(self, k, level):
        core, first, second = self.bits
        n = 4 * k + level
        if level == 0:
            return self.remote(n, self.give.at[k], self.got0.at[k], CORE)
        if level == 1:
            begin, rows = self.quarter(1 - first)
            return self.remote(n, self.keep.at[k, pl.ds(begin, rows), :], self.got1.at[k], self.first)
        if level == 2:
            return self.remote(n, self.part(self.keep.at[k], self.eighth(first, 1 - second)), self.got2.at[k], self.second)
        return self.remote(n, self.part(self.keep.at[k], self.eighth(first, second)), self.got_tp.at[k - 1], 0, k)

    def share(self, n):
        first, second = self.first, self.second
        bits, source = (
            (first, (0, 0, 0)), (second, (0, 0, 0)), (first | second, (0, 0, 0)), (CORE, (0, 0, 0)),
            (CORE, (0, 1, 0)), (CORE, (0, 0, 1)), (CORE, (0, 1, 1)),
        )[n]
        place = self.place(source)
        return self.remote(16 + n, self.total if n < 4 else place, place, bits)

    def add(self, target, begin, rows, columns, *items):
        step = 48

        def body(i, carry):
            here = pl.ds(pl.multiple_of(begin + i * step, 16), step)
            there = pl.ds(pl.multiple_of(i * step, 16), step)
            if len(items) == 1:
                target[here, columns] = target[here, columns] + items[0][there, :]
            else:
                total = target[here, columns].astype(f32)
                for item in items:
                    total += item[there, :].astype(f32)
                target[here, columns] = total.astype(bf16)
            return carry

        lax.fori_loop(0, rows // step, body, 0)

    def step0(self, k):
        self.copy(k, 0).start()

    def given(self, k):
        self.copy(k, 0).wait_send()

    def step1(self, k):
        self.copy(k, 0).wait_recv()
        self.add(self.keep.at[k], 0, self.rows // 2, slice(None), self.got0.at[k])
        self.copy(k, 1).start()

    def step2(self, k):
        self.copy(k, 1).wait_recv()
        begin, rows = self.quarter(self.bits[1])
        self.add(self.keep.at[k], begin, rows, slice(None), self.got1.at[k])
        self.copy(k, 2).start()

    def step3(self, k):
        self.copy(k, 2).wait_recv()
        self.add(self.keep.at[k], *self.eighth(*self.bits[1:]), self.got2.at[k])
        if k:
            self.copy(k, 3).start()

    def step4(self):
        for k in (1, 2, 3):
            self.copy(k, 3).wait_recv()
        begin, rows, columns = self.eighth(*self.bits[1:])
        self.add(self.keep.at[0], begin, rows, columns, *[self.got_tp.at[k] for k in range(3)])
        self.total[...] = self.keep[0, pl.ds(begin, rows), columns]
        for n in range(4):
            self.share(n).start()
        self.own_copy().start()

    def own_copy(self):
        return pltpu.make_async_copy(self.total, self.place((0, 0, 0)), self.own_sem)

    def step5(self):
        for n in range(3):
            self.share(n).wait_recv()
            self.share(4 + n).start()

    def step6(self, lowest=0):
        for n in range(3, 7):
            self.share(n).wait_recv()
        for n in range(7):
            self.share(n).wait_send()
        for k in range(4):
            for level in range(lowest, 4 if k else 3):
                self.copy(k, level).wait_send()
        self.own_copy().wait()


VECTORS = 24
UNIT_ROW, HEAD_ROW = 9, 13


VECTOR = 4
BACK_PLAN = {
    (3, 0): ((DOWN, 0, 1),),
    (4, 1): ((DOWN, 1, 1), (DOWN, 2, 1),),
    (4, 3): ((DOWN, 3, 1),),
    (5, 3): ((DOWN, 0, 2), (UP, 0, 1),),
    (6, 1): ((DOWN, 1, 2),),
    (6, 3): ((UP, 1, 1), (DOWN, 0, 3),),
    (7, 1): ((DOWN, 2, 2),),
    (7, 3): ((UP, 2, 1), (UP, 0, 2),),
    (8, 1): ((DOWN, 1, 3), (DOWN, 3, 2), (UP, 3, 1), (UP, 0, 3), (UP, 1, 2),),
    (8, 3): ((DOWN, 2, 3), (PROJ, 1, 1),),
    (8, 7): ((UP, 2, 2), (UP, 1, 3),),
    (9, 1): ((DOWN, 3, 3), (HEADS, 1, 1),),
    (9, 3): ((PROJ, 2, 1), (UP, 2, 3),),
    (9, 6): ((UP, 3, 2), (PROJ, 1, 2),),
    (9, 7): ((PROJ, 2, 2),),
    (10, 1): ((HEADS, 1, 2), (DOWN, 0, 4), (HEADS, 2, 1), (UP, 3, 3),),
    (10, 3): ((PROJ, 1, 3), (PROJ, 3, 1), (PROJ, 2, 3),),
    (10, 6): ((HEADS, 1, 3),),
    (11, 1): ((UP, 0, 4), (HEADS, 3, 1), (DOWN, 0, 5),),
    (11, 3): ((PROJ, 3, 2), (PROJ, 0, 1), (HEADS, 2, 2),),
    (12, 1): ((UP, 0, 5), (PROJ, 0, 2),),
    (12, 2): ((HEADS, 0, 1),),
}
BACK_TAIL = (
    (HEADS, 2, 3),
    (HEADS, 3, 2),
    (PROJ, 3, 3),
    (PROJ, 0, 3),
    (VECTOR, 0, 0),
    (HEADS, 3, 3),
    (HEADS, 0, 2),
    (VECTOR, 1, 0),
    (PROJ, 0, 4),
    (HEADS, 0, 3),
    (HEADS, 0, 4),
    (VECTOR, 2, 0),
    (PROJ, 0, 5),
    (HEADS, 0, 5),
)


def back_kernel(
    grad_low_ref, hidden_ref, slope_ref, down_ref, up_ref, normed2_ref, middle_ref, grad_out_ref,
    inputs_ref, normed1_ref, packed_ref, mixed_ref, lse_ref, heads_ref, proj_ref, column_ref, row_ref, flag_ref,
    constants_ref, sums_ref,
    grad_inputs_ref, vector_ref, out_down, out_up, out_heads, out_proj,
    grad_unit, total, flipped, grad_mixed, grad_packed, delta, grad_query,
    keep_down, keep_up, keep_heads, keep_proj, give_down, give_heads, give_proj,
    vectors, vector_got, vector_tp, vector_sends, vector_recvs, own_sems,
    *rest,
):
    slots, width = normed2_ref.shape
    triple = heads_ref.shape[2] // 3
    size = triple // 3
    scale = size ** (-0.5)
    step = pl.program_id(0)
    got, sems = [rest[5 * n:5 * n + 5] for n in range(4)], rest[20:]
    give_up = give_down
    constant = lambda n: constants_ref[n:n + 1, :]
    make = lambda n, first, second, by_columns, keep, give, out: Reduce(
        first, second, by_columns, keep, give, got[n], out, sems[2 * n], sems[2 * n + 1], own_sems.at[n])
    down = make(0, X, Y, False, keep_down, give_down, out_down)
    up = make(1, Y, X, False, keep_up, give_up, out_up)
    heads = make(2, X, Y, False, keep_heads, give_heads, out_heads)
    proj = make(3, Y, X, True, keep_proj, give_proj, out_proj)
    dp, tp, core = down.dp, down.tp, down.bits[0]
    n_dp = lax.axis_size("dp")
    levels = [bit for bit in (1, 2, 4, 8, 16, 32, 64, 128) if bit < n_dp]

    def vector_copy(n):
        if n < len(levels):
            return heads_like(vectors.at[n], vector_got.at[n], n, levels[n], 0)
        k = n - len(levels) + 1
        return heads_like(vectors.at[len(levels)], vector_tp.at[k - 1], n, 0, k)

    def heads_like(source, target, n, bits, k):
        return pltpu.make_async_remote_copy(
            src_ref=source, dst_ref=target, send_sem=vector_sends.at[n], recv_sem=vector_recvs.at[n],
            device_id=(flip(dp, bits), flip(tp, k)), device_id_type=pl.DeviceIdType.MESH,
        )

    def vector_step(n):
        vector_copy(n).wait_recv()
        vectors[n + 1] = vectors[n] + vector_got[n]
        if n + 1 < len(levels):
            vector_copy(n + 1).start()
        else:
            for k in (1, 2, 3):
                vector_copy(len(levels) + k - 1).start()

    def action_of(entry):
        item, k, part = entry
        if item == VECTOR:
            return functools.partial(vector_step, k)
        item = {HEADS: heads, UP: up, PROJ: proj, DOWN: down}[item]
        if part > 3:
            return (item.step4, item.step5)[part - 4]
        return functools.partial((item.step1, item.step2, item.step3)[part - 1], k)

    table = {key: [action_of(entry) for entry in entries] for key, entries in BACK_PLAN.items()}
    tail = [action_of(entry) for entry in BACK_TAIL]
    tail += [functools.partial(vector_step, n) for n in range(3, len(levels))]

    def pump(steps, unit):
        for at in steps:
            if (at, unit) in table:

                @pl.when(step == at)
                def _():
                    for action in table[(at, unit)]:
                        action()

    def each_send(item, place, steps):
        for k, at in steps:

            @pl.when(step == at)
            def _():
                item.step0(k)

    halves_of = (pl.ds(pl.multiple_of(core * (width // 2), 128), width // 2),
                 pl.ds(pl.multiple_of((1 - core) * (width // 2), 128), width // 2))

    @pl.when(step == 0)
    def _():
        vectors[0] = jnp.zeros_like(vectors[0])
        vectors[0, 7:8, :] = sums_ref[1:2, :]
        vectors[0, 8:9, :] = sums_ref[0:1, :]
        peers = [(dp, flip(tp, k)) for k in (1, 2, 3)]
        peers += [(flip(dp, bits), tp) for bits in (X, Y, X | Y, CORE)]
        peers += [(flip(dp, bit), tp) for bit in levels if bit >= 8]
        meet(peers)

    @pl.when(step < 4)
    def _():
        keep_down[step] = dot(hidden_ref[0, :, halves_of[0]], grad_low_ref[...], TN).astype(bf16)
        give_down[step] = dot(hidden_ref[0, :, halves_of[1]], grad_low_ref[...], TN).astype(bf16)
        each_send(down, 0, [(k, k) for k in range(4)])
        pump(range(4), 0)

    @pl.when(step == 4)
    def _():
        total[...] = jnp.zeros_like(total)
        flipped[...] = normed2_ref[...].T

    @pl.when(jnp.logical_and(step >= 4, step < 8))
    def _():
        unit_sum = jnp.zeros((1, slope_ref.shape[2]), f32)
        for n, (low, high) in enumerate(rows_of(slots, 208)):
            unit = dot(grad_low_ref[low:high, :], down_ref[0], NT) * slope_ref[0, low:high, :].astype(f32)
            unit = unit.astype(bf16)
            grad_unit[low:high, :] = unit
            unit_sum += jnp.sum(unit.astype(f32), axis=0, keepdims=True)
            total[low:high, :] += dot(unit, up_ref[0], NT)
            pump(range(4, 8), n)
        k = step - 4
        for at in range(4):

            @pl.when(k == at)
            def _():
                vectors[0, UNIT_ROW + at:UNIT_ROW + at + 1, :] = unit_sum
        keep_up[k] = dot(flipped[halves_of[0], :], grad_unit[...]).astype(bf16)
        for at in range(4):

            @pl.when(k == at)
            def _():
                down.given(at)
        give_up[k] = dot(flipped[halves_of[1], :], grad_unit[...]).astype(bf16)
        each_send(up, 0, [(k, 4 + k) for k in range(4)])
        pump(range(4, 8), 4)

    @pl.when(step == 7)
    def _():
        gain, attn_scale = constant(GAIN2), constant(ATTN_SCALE)

        def body(i, sums):
            here = pl.ds(pl.multiple_of(i * 64, 64), 64)
            valid, _, start = start_of(inputs_ref, column_ref, flag_ref, constant(TOKEN), here)
            grad_final = valid * grad_out_ref[here, :].astype(f32)
            grad_normed = total[here, :]
            _, scaled, inverse = layer_norm(middle_ref[here, :], gain, gain)
            grad_middle = grad_final + norm_back(grad_normed, scaled, inverse, gain)
            grad_branch1 = attn_scale * grad_middle
            grad_inputs_ref[here, :] = grad_middle
            grad_unit[here, :] = grad_branch1.astype(bf16)
            new = (grad_branch1, (middle_ref[here, :] - start) / attn_scale * grad_middle, grad_normed * scaled, grad_normed)
            return tuple(a + jnp.sum(b, axis=0, keepdims=True) for a, b in zip(sums, new))

        zero = jnp.zeros((1, width), f32)
        sums = lax.fori_loop(0, slots // 64, body, (zero,) * 4)
        for n in range(4):
            vectors[0, 3 + n:4 + n, :] = sums[n]
        total[...] = jnp.zeros_like(total)
        flipped[...] = normed1_ref[...].T

    attending = range(8, 12)
    shard_of = {8: 1, 9: 2, 10: 3, 11: 0}

    @pl.when(jnp.logical_and(step >= 8, step < 12))
    def _():
        k = lax.rem(step - 7, 4)
        grad_low1 = grad_unit
        for low in range(0, slots, 208):
            grad_mixed[low:low + 208, :] = dot(grad_low1[low:low + 208, :], proj_ref[0], NT).astype(bf16)
        value = dot(mixed_ref[0], grad_low1[...], TN).astype(bf16)
        rows = value.shape[0] // 2
        for own in (0, 1):

            @pl.when(core == own)
            def _():
                keep_proj[k] = value[own * rows:(own + 1) * rows]
                give_proj[k] = value[(1 - own) * rows:(2 - own) * rows]
        each_send(proj, 0, [(shard_of[at], at) for at in attending])
        tiles = windows(slots)
        bases = [head * triple for head in range(3)]
        owns = [slice(head * size, (head + 1) * size) for head in range(3)]
        for low, high, _, _ in tiles:
            for head, own in enumerate(owns):
                product = grad_mixed[low:high, own].astype(f32) * mixed_ref[0, low:high, own].astype(f32)
                delta[head:head + 1, low:high] = as_row(jnp.sum(product, axis=1, keepdims=True))
        grad_query[...] = jnp.zeros_like(grad_query)
        for unit, (low, high, begin, end) in enumerate(tiles):
            same = column_ref[low:high, :] == row_ref[:, begin:end]
            keys = [packed_ref[0, low:high, base + size:base + 2 * size] for base in bases]
            queries = [packed_ref[0, begin:end, base:base + size] * jnp.bfloat16(scale) for base in bases]
            grads = [grad_mixed[begin:end, own] for own in owns]
            scores = [dot(key, query, NT) for key, query in zip(keys, queries)]
            grad_shares = [
                dot(packed_ref[0, low:high, base + 2 * size:base + 3 * size], grad, NT)
                for base, grad in zip(bases, grads)
            ]
            shares = [
                jnp.exp(jnp.where(same, item - lse_ref[0, head:head + 1, begin:end], FLOOR_SCORE))
                for head, item in enumerate(scores)
            ]
            grad_scores = [
                (share * (item - delta[head:head + 1, begin:end])).astype(bf16)
                for head, (share, item) in enumerate(zip(shares, grad_shares))
            ]
            for head, base in enumerate(bases):
                grad_packed[low:high, base + size:base + 3 * size] = jnp.concatenate([
                    dot(grad_scores[head], queries[head]).astype(bf16),
                    dot(shares[head].astype(bf16), grads[head]).astype(bf16),
                ], axis=1)
                grad_query[head, begin:end, :] += dot(grad_scores[head], keys[head], TN)
            pump(attending, unit)
        for head, base in enumerate(bases):
            grad_packed[:, base:base + size] = (grad_query[head] * scale).astype(bf16)
        keep_heads[k] = dot(flipped[halves_of[0], :], grad_packed[...]).astype(bf16)
        give_heads[k] = dot(flipped[halves_of[1], :], grad_packed[...]).astype(bf16)
        each_send(heads, 0, [(shard_of[at], at) for at in attending])
        sums = jnp.sum(grad_packed[...].astype(f32), axis=0, keepdims=True)
        for at in range(4):

            @pl.when(k == at)
            def _():
                vectors[0, HEAD_ROW + at:HEAD_ROW + at + 1, :sums.shape[1]] = sums
        for low in range(0, slots, 208):
            total[low:low + 208, :] += dot(grad_packed[low:low + 208, :], heads_ref[0], NT)
        pump(attending, 7)

    @pl.when(step == 12)
    def _():
        gain = constant(GAIN1)

        def body(i, sums):
            here = pl.ds(pl.multiple_of(i * 64, 64), 64)
            valid, flagged, start = start_of(inputs_ref, column_ref, flag_ref, constant(TOKEN), here)
            _, scaled, inverse = layer_norm(start, gain, gain)
            grad_normed = total[here, :]
            grad_start = grad_inputs_ref[here, :] + norm_back(grad_normed, scaled, inverse, gain)
            grad_inputs_ref[here, :] = valid * (1.0 - flagged) * grad_start
            new = (valid * flagged * grad_start, grad_normed * scaled, grad_normed)
            return tuple(a + jnp.sum(b, axis=0, keepdims=True) for a, b in zip(sums, new))

        zero = jnp.zeros((1, width), f32)
        sums = (zero,) * 3
        for n, (low, high) in enumerate(((0, 4), (4, 8), (8, slots // 64))):
            sums = lax.fori_loop(low, high, body, sums)
            pump((12,), n)
        for n in range(3):
            vectors[0, n:n + 1, :] = sums[n]
        vector_copy(0).start()
        pump((12,), 3)
        for action in tail:
            action()
        last_level = len(levels)
        for k in (1, 2, 3):
            vector_copy(last_level + k - 1).wait_recv()
        mine = vectors[last_level]
        vector_ref[...] = mine + vector_tp[0] + vector_tp[1] + vector_tp[2]
        for row_at in (UNIT_ROW, HEAD_ROW):
            value = mine[row_at:row_at + 1]
            for k in (1, 2, 3):
                value += vector_tp[k - 1, row_at + k:row_at + k + 1, :]
            vector_ref[row_at:row_at + 1, :] = value
        for n in range(last_level + 3):
            vector_copy(n).wait_send()
        down.step6(1)
        for item in (up, heads, proj):
            item.step6()


def back(grad_low, hidden, slope, down, up, normed2, middle, grad_out, inputs, normed1, packed, mixed, lse,
         heads, proj, column, row, flag, constants, sums):
    slots, width = normed2.shape
    units, columns, part = hidden.shape[2], heads.shape[2], mixed.shape[2]
    levels = lax.axis_size("dp").bit_length() - 1
    clip = lambda low, high: lambda at: jnp.minimum(jnp.maximum(at, low), high)
    in_down, in_up = clip(0, 3), lambda at: clip(4, 7)(at) - 4
    in_heads = lambda at: lax.rem(clip(8, 11)(at) - 7, 4)
    tokens, anywhere = once(slots, width), pl.BlockSpec(memory_space=pl.ANY)
    shapes = [(units, width), (width, units), (width, columns), (part, width)]
    got = []
    for n, (rows, cols) in enumerate(shapes):
        eighth = (rows // 4, cols // 2) if n == 3 else (rows // 8, cols)
        got += [pltpu.VMEM((4, rows // 2, cols), bf16), pltpu.VMEM((4, rows // 4, cols), bf16),
                pltpu.VMEM((4,) + eighth, bf16), pltpu.VMEM((3,) + eighth, bf16), pltpu.VMEM(eighth, bf16)]
    half = [pltpu.VMEM((4, rows // 2, cols), bf16) for rows, cols in shapes]
    return pl.pallas_call(
        back_kernel,
        grid=(13,),
        in_specs=[
            tokens, each(slots, units, at=in_down), each(slots, units, at=in_up), each(units, width, at=in_up),
            each(width, units, at=in_up), tokens, tokens, tokens, tokens, tokens,
            each(slots, columns, at=in_heads), each(slots, part, at=in_heads), each(8, slots, at=in_heads),
            each(width, columns, at=in_heads), each(part, width, at=in_heads), once(slots, 1), once(1, slots),
            once(slots, 1), once(*constants.shape), once(8, width),
        ],
        out_specs=[once(slots, width), once(VECTORS, width), anywhere, anywhere, anywhere, anywhere],
        out_shape=[jax.ShapeDtypeStruct((slots, width), f32), jax.ShapeDtypeStruct((VECTORS, width), f32)]
        + [jax.ShapeDtypeStruct(shape, bf16) for shape in shapes],
        scratch_shapes=[
            pltpu.VMEM((slots, units), bf16), pltpu.VMEM((slots, width), f32), pltpu.VMEM((width, slots), bf16),
            pltpu.VMEM((slots, part), bf16), pltpu.VMEM((slots, columns), bf16), pltpu.VMEM((8, slots), f32),
            pltpu.VMEM((3, slots, columns // 9), f32),
        ] + half + [half[0]] + half[2:] + [
            pltpu.VMEM((levels + 1, VECTORS, width), f32), pltpu.VMEM((levels, VECTORS, width), f32),
            pltpu.VMEM((3, VECTORS, width), f32), pltpu.SemaphoreType.DMA((levels + 3,)),
            pltpu.SemaphoreType.DMA((levels + 3,)), pltpu.SemaphoreType.DMA((4,)),
        ] + got + [pltpu.SemaphoreType.DMA((Reduce.COPIES,))] * 8,
        compiler_params=pltpu.CompilerParams(vmem_limit_bytes=65400 << 10, collective_id=1, has_side_effects=True),
        cost_estimate=cost(36e9, 60e6, 12 * 480000),
        name="back",
    )(grad_low, hidden, slope, down, up, normed2, middle, grad_out, inputs, normed1, packed, mixed, lse,
      heads, proj, column, row, flag, constants, sums)


def local(
    inputs,
    segment_ids,
    mask_flags,
    mask_token,
    norm_gain,
    norm_shift,
    heads_weight,
    heads_bias,
    proj_weight,
    proj_bias,
    attn_scale,
    mlp_gain,
    mlp_shift,
    up_weight,
    up_bias,
    down_weight,
    down_bias,
    mlp_scale,
    grad_out,
):
    width = inputs.shape[1]
    triple = heads_weight.shape[2]
    head_size = triple // 3
    heads_here = heads_weight.shape[1]
    own_heads = heads_weight.reshape(width, -1)
    heads_cols = own_heads.shape[1]
    constants = jnp.concatenate([
        mask_token, norm_gain, norm_shift, proj_bias, attn_scale, mlp_gain, mlp_shift, down_bias, mlp_scale,
        jnp.zeros((7 * width,), bf16)]).astype(f32).reshape(16, width)
    (normed1, column, flag, row, packed, mixed, lse, middle, normed2, hidden, slope, output, grad_low2, sums_a,
     heads_all, up_all, proj_all, down_all) = forward(
        inputs, segment_ids, mask_flags, constants, heads_bias, up_bias.reshape(1, -1), grad_out, own_heads, up_weight,
        proj_weight, down_weight,
    )
    grad_inputs, small, sum_down, sum_up, sum_heads, sum_proj = back(
        grad_low2, hidden, slope, down_all, up_all, normed2, middle, grad_out, inputs, normed1, packed, mixed,
        lse, heads_all, proj_all, column, row, flag, constants, sums_a,
    )
    sum_down, sum_up, sum_proj = (item.astype(f32) for item in (sum_down, sum_up, sum_proj))
    sum_heads = sum_heads.astype(f32).reshape(heads_weight.shape)
    bias_sums = small[HEAD_ROW, :heads_cols].reshape(heads_here, triple)
    sum_heads_bias = jnp.concatenate([bias_sums[:, :head_size], bias_sums[:, 2 * head_size:]], axis=1)
    sum_up_bias = small[UNIT_ROW, :up_bias.shape[0]]
    (sum_token, sum_gain1, sum_shift1, sum_proj_bias, sum_scale1, sum_gain2, sum_shift2,
     sum_down_bias, sum_scale2) = [small[i] for i in range(9)]
    return (
        output,
        grad_inputs,
        sum_token,
        sum_gain1,
        sum_shift1,
        sum_heads,
        sum_heads_bias,
        sum_proj,
        sum_proj_bias,
        sum_scale1,
        sum_gain2,
        sum_shift2,
        sum_up,
        sum_up_bias,
        sum_down,
        sum_down_bias,
        sum_scale2,
    )


def solution(mesh):
    placed = (
        P(("dp", "tp"), None),
        P("dp", None),
        P(("dp", "tp"), None),
        P(),
        P(),
        P(),
        P(None, "tp", None),
        P("tp", None),
        P("tp", None),
        P(),
        P(),
        P(),
        P(),
        P(None, "tp"),
        P("tp"),
        P("tp", None),
        P(),
        P(),
        P(("dp", "tp"), None),
    )
    return jax.shard_map(
        local,
        mesh=mesh,
        in_specs=placed,
        out_specs=(
            P(("dp", "tp"), None),
            P(("dp", "tp"), None),
            P(),
            P(),
            P(),
            P(None, "tp", None),
            P("tp", None),
            P("tp", None),
            P(),
            P(),
            P(),
            P(),
            P(None, "tp"),
            P("tp"),
            P("tp", None),
            P(),
            P(),
        ),
        check_vma=False,
    )
```

time: 289 us -> 236 us (0.82)
  Pallas kernels: 251 us -> 207 us
  starting transfers between devices: 5.7 us -> 0 us
    pallas_call x1, Pallas kernels: 159 us -> 124 us  [back(): pl.pallas_call(back_kernel, grid=(13,), in_specs=[tokens, each(slots, uni...]
    pallas_call x2 -> x1, Pallas kernels: 92.2 us -> 82.8 us  [forward(): pl.pallas_call(forward_kernel, grid=(8,), in_specs=[tokens, once(*segment...]
    ppermute x3 -> x0, starting transfers between devices: 5.7 us -> none  [exchange(): return lax.ppermute(value, ('dp', 'tp'), pairs)]
    unnamed x61 -> x19, local copies, waits for them, and re-layouts: 12.1 us -> 11.6 us
  transfers between devices with their start and end apart: 3 -> 0, of which waited for: 0 -> 0; matrix products, arithmetic and copies ran while one was open for 2% -> 0% of each run, Pallas kernels for 0% -> 0%
where the time goes in v1:
time: 236 us; the launch traced here: 235 us
  Pallas kernels  207 us (88%)
  local copies, waits for them, and re-layouts  21.2 us (9%)
  other arithmetic  5.72 us (2%)
    pallas_call x1, Pallas kernels, back(): pl.pallas_call(back_kernel, grid=(13,), in_specs=[tokens, each(slots, uni...  124 us
    pallas_call x1, Pallas kernels, forward(): pl.pallas_call(forward_kernel, grid=(8,), in_specs=[tokens, once(*segment...  82.8 us
    unnamed x19, local copies, waits for them, and re-layouts  11.6 us
    convert_element_type x3, other arithmetic, local(): item.astype(f32)  5.06 us

profile of v1, /device:TPU:0, one launch (start us, length us, event | category | flops | bytes accessed | tf_op | source)
XLA Modules:
  0.0 234.7 jit_solution(3015085463194233680)
XLA Ops:
  0.7 1.3 reshape.50.unit_bias_ref
  1.9 0.8 dynamic-update-slice
  2.8 0.8 dynamic-update-slice.1
  3.6 0.9 dynamic-update-slice.2
  4.5 0.9 dynamic-update-slice.3
  5.3 0.9 dynamic-update-slice.4
  6.2 0.8 dynamic-update-slice.5
  7.0 0.9 dynamic-update-slice.6
  7.9 0.9 dynamic-update-slice.7
  8.7 0.9 dynamic-update-slice.8
  9.6 0.3 dynamic-update-slice.9
  9.9 0.7 reshape.54.vectors_ref.constants_ref
  10.5 2.2 copy.38.heads_ref
  12.8 82.8 %forward.1 = (bf16[832,768]{1,0:T(8,128)(2,1)}, s32[832,1]{1,0:T(8,128)}, s32[832,1]{1,0:T(8,128)}, s32[1,832]{1,0:T(1,128)}, bf16[4,832,576]{2,1,0:T(8,128)(2,1...) custom-call(bf16[832,768]{1,0:T(8,128)(2,1)} %inputs_ref.3, ...), custom_call_target="tpu_custom_call" | custom-call | flops 25999998976 | bytes 60000000 | tf_op jit(solution)/shard_map/forward/pallas_call | solution.py:422
  95.6 124.3 %back.1 = (f32[832,768]{1,0:T(8,128)}, f32[24,768]{1,0:T(8,128)}, bf16[768,768]{1,0:T(8,128)(2,1)}, bf16[768,768]{1,0:T(8,128)(2,1)}, bf16[768,576]{1,0:T(8,128)(2,1)}, /*index=5*/bf16[192,768]{1,0:T(8,128)(2,1)}) custom-call(bf16[832,768]{1,0:T(8,128)(2,1)} %get-tuple-element.42.grad_low_ref, bf16[4,832,768]{2,1,0:T(8,128)(2,1)} %get-tuple-element.43.hidden_ref, ...), custom_call_target="tpu_custom_call" | custom-call | flops 35999997952 | bytes 60000000 | tf_op jit(solution)/shard_map/back/pallas_call | solution.py:905
  219.9 0.7 slice_reduce_fusion.10
  220.7 1.9 slice_reduce_fusion
  222.6 0.1 reshape_squeeze.3
  222.6 0.7 pad_maximum_fusion
  223.3 0.0 copy-start.3
  223.3 1.9 convert_element_type.19
  225.2 2.4 %copy.39 = f32[768,576]{0,1:T(8,128)} copy(bf16[768,576]{1,0:T(8,128)(2,1)} %get-tuple-element.61) | data formatting | bytes 2654208 | tf_op jit(solution)/shard_map/reshape | solution.py:974
  227.6 0.0 copy-done.3
  227.6 0.0 copy-start.2
  227.6 1.6 convert_element_type.20
  229.2 0.1 copy-done.2
  229.3 0.0 copy-start.1
  229.3 1.6 convert_element_type.21
  230.9 0.2 copy-done.1
  231.1 0.0 copy-start
  231.1 1.0 copy.52
  232.1 1.1 copy-done
  233.3 1.5 copy.53
  (3 shorter events, 0.0 us)
Async XLA Ops:
  223.3 4.3 %copy-start.3 = (bf16[768,768]{1,0:T(8,128)(2,1)S(1)}, bf16[768,768]{1,0:T(8,128)(2,1)}, u32[]{:S(2)}) copy-start(bf16[768,768]{1,0:T(8,128)(2,1)} %get-tuple-element.63) | copy-start | bytes 3538948
  227.6 1.7 copy-start.2
  229.3 1.8 copy-start.1
  231.1 2.2 copy-start

commit v2 on v1

--- a/solution.py
+++ b/solution.py
@@ -233,14 +233,14 @@
 
 
 def forward_kernel(
-    inputs_ref, segment_ref, mask_ref, vectors_ref, heads_bias_ref, unit_bias_ref, grad_out_ref,
-    heads_ref, up_ref, proj_ref, down_ref,
-    normed1_ref, column_ref, flag_ref, row_ref, packed_ref, mixed_ref, lse_ref, middle_ref, normed2_ref, hidden_ref,
-    slope_ref, output_ref, grad_low_ref, sums_ref, heads_all, up_all, proj_all, down_all,
-    heads_now, up_now, proj_now, down_now, head_bias, unit_bias, mixed_all, total,
-    own_sems, store_sems, bias_sends, bias_recvs,
-    *sems,
+    inputs_ref, segment_ref, mask_ref, heads_bias_ref, unit_bias_ref, grad_out_ref,
+    heads_ref, up_ref, proj_ref, down_ref, *rest,
 ):
+    vector_refs, rest = rest[:9], rest[9:]
+    (normed1_ref, column_ref, flag_ref, row_ref, packed_ref, mixed_ref, lse_ref, middle_ref, normed2_ref, hidden_ref,
+     slope_ref, output_ref, grad_low_ref, sums_ref, vectors_ref, heads_all, up_all, proj_all, down_all,
+     heads_now, up_now, proj_now, down_now, head_bias, unit_bias, mixed_all, total,
+     own_sems, store_sems, bias_sends, bias_recvs, *sems) = rest
     slots = inputs_ref.shape[0]
     triple = heads_now.shape[2] // 3
     size = triple // 3
@@ -281,13 +281,16 @@
         loads[HEADS].wait()
         for k in (1, 2, 3):
             gathers[HEADS].begin(k)
+        vectors_ref[...] = jnp.zeros_like(vectors_ref)
+        for n, ref in enumerate(vector_refs):
+            vectors_ref[n:n + 1, :] = ref[...].astype(f32).reshape(1, -1)
         blank = jnp.zeros((1, size), f32)
         pieces = []
         for head in range(3):
             here = heads_bias_ref[head:head + 1, :].astype(f32)
             pieces += [here[:, :size], blank, here[:, size:]]
         head_bias[0] = jnp.broadcast_to(jnp.concatenate(pieces, axis=1), head_bias.shape[1:])
-        unit_bias[0] = jnp.broadcast_to(unit_bias_ref[...].astype(f32), unit_bias.shape[1:])
+        unit_bias[0] = jnp.broadcast_to(unit_bias_ref[...].astype(f32).reshape(1, -1), unit_bias.shape[1:])
         for n in range(2):
             for k in (1, 2, 3):
                 bias_copy(n, k).start()
@@ -423,20 +426,20 @@
         forward_kernel,
         grid=(8,),
         in_specs=[
-            tokens, once(*segments.shape), once(1, slots), once(*vectors.shape), once(*heads_bias.shape),
+            tokens, once(*segments.shape), once(1, slots), once(*heads_bias.shape),
             once(*unit_bias.shape), tokens, anywhere, anywhere, anywhere, anywhere,
-        ],
+        ] + [once(width)] * len(vectors),
         out_specs=[
             tokens, once(slots, 1), once(slots, 1), once(1, slots), each(slots, columns, at=early),
             each(slots, part, at=early), each(8, slots, at=early), tokens, tokens, each(slots, units, at=late),
-            each(slots, units, at=late), tokens, tokens, once(8, width), anywhere, anywhere, anywhere, anywhere,
+            each(slots, units, at=late), tokens, tokens, once(8, width), once(16, width), anywhere, anywhere, anywhere, anywhere,
         ],
         out_shape=[
             shape((slots, width), bf16), shape((slots, 1), jnp.int32), shape((slots, 1), jnp.int32),
             shape((1, slots), jnp.int32), shape((4, slots, columns), bf16), shape((4, slots, part), bf16),
             shape((4, 8, slots), f32), shape((slots, width), f32), shape((slots, width), bf16),
             shape((4, slots, units), bf16), shape((4, slots, units), bf16), shape((slots, width), bf16),
-            shape((slots, width), bf16), shape((8, width), f32),
+            shape((slots, width), bf16), shape((8, width), f32), shape((16, width), f32),
         ] + [shape((4,) + item.shape, bf16) for item in (heads, up, proj, down)],
         scratch_shapes=[
             pltpu.VMEM((4,) + heads.shape, bf16), pltpu.VMEM((4,) + up.shape, bf16), pltpu.VMEM((4,) + proj.shape, bf16),
@@ -447,7 +450,7 @@
         compiler_params=pltpu.CompilerParams(vmem_limit_bytes=60 << 20, collective_id=0, has_side_effects=True),
         cost_estimate=cost(26e9, 60e6, 6e6),
         name="forward",
-    )(inputs, segments, mask, vectors, heads_bias, unit_bias, grad_out, heads, up, proj, down)
+    )(inputs, segments, mask, heads_bias, unit_bias, grad_out, heads, up, proj, down, *vectors)
 
 
 class Reduce:
@@ -958,12 +961,10 @@
     heads_here = heads_weight.shape[1]
     own_heads = heads_weight.reshape(width, -1)
     heads_cols = own_heads.shape[1]
-    constants = jnp.concatenate([
-        mask_token, norm_gain, norm_shift, proj_bias, attn_scale, mlp_gain, mlp_shift, down_bias, mlp_scale,
-        jnp.zeros((7 * width,), bf16)]).astype(f32).reshape(16, width)
+    vectors = (mask_token, norm_gain, norm_shift, proj_bias, attn_scale, mlp_gain, mlp_shift, down_bias, mlp_scale)
     (normed1, column, flag, row, packed, mixed, lse, middle, normed2, hidden, slope, output, grad_low2, sums_a,
-     heads_all, up_all, proj_all, down_all) = forward(
-        inputs, segment_ids, mask_flags, constants, heads_bias, up_bias.reshape(1, -1), grad_out, own_heads, up_weight,
+     constants, heads_all, up_all, proj_all, down_all) = forward(
+        inputs, segment_ids, mask_flags, vectors, heads_bias, up_bias, grad_out, own_heads, up_weight,
         proj_weight, down_weight,
     )
     grad_inputs, small, sum_down, sum_up, sum_heads, sum_proj = back(

time: 236 us -> 225 us (0.953)
  local copies, waits for them, and re-layouts: 21.2 us -> 11.3 us
    unnamed x19 -> x10, local copies, waits for them, and re-layouts: 11.6 us -> 3.95 us
where the time goes in v2:
time: 225 us; the launch traced here: 224 us
  Pallas kernels  206 us (92%)
  local copies, waits for them, and re-layouts  11.3 us (5%)
  other arithmetic  5.72 us (3%)
    pallas_call x1, Pallas kernels, back(): pl.pallas_call(back_kernel, grid=(13,), in_specs=[tokens, each(slots, uni...  123 us
    pallas_call x1, Pallas kernels, forward(): pl.pallas_call(forward_kernel, grid=(8,), in_specs=[tokens, once(*segment...  83 us
    convert_element_type x3, other arithmetic, local(): item.astype(f32)  5.06 us

profile of v2, /device:TPU:0, one launch (start us, length us, event | category | flops | bytes accessed | tf_op | source)
XLA Modules:
  0.0 223.9 jit_solution(8557384554714147378)
XLA Ops:
  0.7 2.2 copy.38.heads_ref
  2.9 83.0 %forward.1 = (bf16[832,768]{1,0:T(8,128)(2,1)}, s32[832,1]{1,0:T(8,128)}, s32[832,1]{1,0:T(8,128)}, s32[1,832]{1,0:T(1,128)}, bf16[4,832,576]{2,1,0:T(8,128)(2,1...) custom-call(bf16[832,768]{1,0:T(8,128)(2,1)} %inputs_ref.3, ...), custom_call_target="tpu_custom_call" | custom-call | flops 25999998976 | bytes 60000000 | tf_op jit(solution)/shard_map/forward/pallas_call | solution.py:425
  85.9 123.1 %back.1 = (f32[832,768]{1,0:T(8,128)}, f32[24,768]{1,0:T(8,128)}, bf16[768,768]{1,0:T(8,128)(2,1)}, bf16[768,768]{1,0:T(8,128)(2,1)}, bf16[768,576]{1,0:T(8,128)(2,1)}, /*index=5*/bf16[192,768]{1,0:T(8,128)(2,1)}) custom-call(bf16[832,768]{1,0:T(8,128)(2,1)} %get-tuple-element.43.grad_low_ref, bf16[4,832,768]{2,1,0:T(8,128)(2,1)} %get-tuple-element.44.hidden_ref, ...), custom_call_target="tpu_custom_call" | custom-call | flops 35999997952 | bytes 60000000 | tf_op jit(solution)/shard_map/back/pallas_call | solution.py:908
  209.1 0.7 slice_reduce_fusion.10
  209.8 1.9 slice_reduce_fusion
  211.7 0.1 reshape_squeeze.3
  211.8 0.7 pad_maximum_fusion
  212.4 0.0 copy-start.3
  212.4 1.9 convert_element_type.10
  214.3 2.4 %copy.39 = f32[768,576]{0,1:T(8,128)} copy(bf16[768,576]{1,0:T(8,128)(2,1)} %get-tuple-element.63) | data formatting | bytes 2654208 | tf_op jit(solution)/shard_map/reshape | solution.py:975
  216.8 0.0 copy-done.3
  216.8 0.0 copy-start.2
  216.8 1.6 convert_element_type.11
  218.3 0.1 copy-done.2
  218.4 0.0 copy-start.1
  218.4 1.6 convert_element_type.12
  220.0 0.2 copy-done.1
  220.2 0.0 copy-start
  220.2 1.0 copy.42
  221.3 1.1 copy-done
  222.4 1.5 copy.43
  (1 shorter events, 0.0 us)
Async XLA Ops:
  212.4 4.3 %copy-start.3 = (bf16[768,768]{1,0:T(8,128)(2,1)S(1)}, bf16[768,768]{1,0:T(8,128)(2,1)}, u32[]{:S(2)}) copy-start(bf16[768,768]{1,0:T(8,128)(2,1)} %get-tuple-element.65) | copy-start | bytes 3538948
  216.8 1.7 copy-start.2
  218.4 1.8 copy-start.1
  220.2 2.2 copy-start

commit v3 on v2

--- a/solution.py
+++ b/solution.py
@@ -301,12 +301,12 @@
             flag_ref[low:high, :] = as_column(mask_ref[:, low:high])
 
         def body(i, carry):
-            here = pl.ds(pl.multiple_of(i * 64, 64), 64)
+            here = pl.ds(pl.multiple_of(i * 208, 16), 208)
             _, _, start = start_of(inputs_ref, column_ref, flag_ref, vector(TOKEN), here)
             normed1_ref[here, :] = layer_norm(start, vector(GAIN1), vector(SHIFT1))[0].astype(bf16)
             return carry
 
-        lax.fori_loop(0, slots // 64, body, 0)
+        lax.fori_loop(0, slots // 208, body, 0)
         for load in loads[1:]:
             load.wait()
         for n in range(4):
@@ -363,14 +363,14 @@
             middle_ref[low:high, :] = dot(mixed_all[low:high, :], proj) + vector(PROJ_BIAS)
 
         def body(i, carry):
-            here = pl.ds(pl.multiple_of(i * 64, 64), 64)
+            here = pl.ds(pl.multiple_of(i * 208, 16), 208)
             _, _, start = start_of(inputs_ref, column_ref, flag_ref, vector(TOKEN), here)
             middle = start + vector(ATTN_SCALE) * middle_ref[here, :]
             middle_ref[here, :] = middle
             normed2_ref[here, :] = layer_norm(middle, vector(GAIN2), vector(SHIFT2))[0].astype(bf16)
             return carry
 
-        lax.fori_loop(0, slots // 64, body, 0)
+        lax.fori_loop(0, slots // 208, body, 0)
 
     @pl.when(step >= 4)
     def _():
@@ -387,7 +387,7 @@
     @pl.when(step == 7)
     def _():
         def body(i, sums):
-            here = pl.ds(pl.multiple_of(i * 64, 64), 64)
+            here = pl.ds(pl.multiple_of(i * 208, 16), 208)
             valid = (column_ref[here, :] >= 0).astype(f32)
             branch2 = total[here, :] + vector(DOWN_BIAS)
             output_ref[here, :] = (valid * (middle_ref[here, :] + vector(MLP_SCALE) * branch2)).astype(bf16)
@@ -397,7 +397,7 @@
             return tuple(a + jnp.sum(b, axis=0, keepdims=True) for a, b in zip(sums, (branch2 * grad_final, grad_branch2)))
 
         zero = jnp.zeros((1, inputs_ref.shape[1]), f32)
-        sums = lax.fori_loop(0, slots // 64, body, (zero, zero))
+        sums = lax.fori_loop(0, slots // 208, body, (zero, zero))
         sums_ref[...] = jnp.zeros_like(sums_ref)
         sums_ref[0:1, :], sums_ref[1:2, :] = sums
         for n, item in enumerate(gathers):

time: 225 us -> 222 us (0.987)
  Pallas kernels: 206 us -> 203 us
    pallas_call x1, Pallas kernels: 83 us -> 80.5 us  [forward(): pl.pallas_call(forward_kernel, grid=(8,), in_specs=[tokens, once(*segment...]
where the time goes in v3:
time: 222 us; the launch traced here: 221 us
  Pallas kernels  203 us (91%)
  local copies, waits for them, and re-layouts  11.3 us (5%)
  other arithmetic  5.72 us (3%)
    pallas_call x1, Pallas kernels, back(): pl.pallas_call(back_kernel, grid=(13,), in_specs=[tokens, each(slots, uni...  122 us
    pallas_call x1, Pallas kernels, forward(): pl.pallas_call(forward_kernel, grid=(8,), in_specs=[tokens, once(*segment...  80.5 us
    convert_element_type x3, other arithmetic, local(): item.astype(f32)  5.06 us

profile of v3, /device:TPU:0, one launch (start us, length us, event | category | flops | bytes accessed | tf_op | source)
XLA Modules:
  0.0 220.7 jit_solution(2335325602662354549)
XLA Ops:
  0.7 2.2 %copy.38.heads_ref = bf16[768,576]{1,0:T(8,128)(2,1)} copy(bf16[768,576]{0,1:T(8,128)(2,1)} %bitcast.3) | data formatting | bytes 1769472 | tf_op jit(solution)/shard_map/reshape | solution.py:962
  2.9 80.5 %forward.1 = (bf16[832,768]{1,0:T(8,128)(2,1)}, s32[832,1]{1,0:T(8,128)}, s32[832,1]{1,0:T(8,128)}, s32[1,832]{1,0:T(1,128)}, bf16[4,832,576]{2,1,0:T(8,128)(2,1...) custom-call(bf16[832,768]{1,0:T(8,128)(2,1)} %inputs_ref.3, ...), custom_call_target="tpu_custom_call" | custom-call | flops 25999998976 | bytes 60000000 | tf_op jit(solution)/shard_map/forward/pallas_call | solution.py:425
  83.4 122.5 %back.1 = (f32[832,768]{1,0:T(8,128)}, f32[24,768]{1,0:T(8,128)}, bf16[768,768]{1,0:T(8,128)(2,1)}, bf16[768,768]{1,0:T(8,128)(2,1)}, bf16[768,576]{1,0:T(8,128)(2,1)}, /*index=5*/bf16[192,768]{1,0:T(8,128)(2,1)}) custom-call(bf16[832,768]{1,0:T(8,128)(2,1)} %get-tuple-element.43.grad_low_ref, bf16[4,832,768]{2,1,0:T(8,128)(2,1)} %get-tuple-element.44.hidden_ref, ...), custom_call_target="tpu_custom_call" | custom-call | flops 35999997952 | bytes 60000000 | tf_op jit(solution)/shard_map/back/pallas_call | solution.py:908
  205.9 0.7 slice_reduce_fusion.10
  206.6 1.9 slice_reduce_fusion
  208.5 0.1 reshape_squeeze.3
  208.6 0.7 pad_maximum_fusion
  209.3 0.0 copy-start.3
  209.3 1.9 convert_element_type.10
  211.2 2.4 %copy.39 = f32[768,576]{0,1:T(8,128)} copy(bf16[768,576]{1,0:T(8,128)(2,1)} %get-tuple-element.63) | data formatting | bytes 2654208 | tf_op jit(solution)/shard_map/reshape | solution.py:975
  213.6 0.0 copy-done.3
  213.6 0.0 copy-start.2
  213.6 1.6 convert_element_type.11
  215.2 0.1 copy-done.2
  215.3 0.0 copy-start.1
  215.3 1.6 convert_element_type.12
  216.8 0.2 copy-done.1
  217.0 0.0 copy-start
  217.1 1.0 copy.42
  218.1 1.1 copy-done
  219.2 1.5 copy.43
  (1 shorter events, 0.0 us)
Async XLA Ops:
  209.3 4.3 %copy-start.3 = (bf16[768,768]{1,0:T(8,128)(2,1)S(1)}, bf16[768,768]{1,0:T(8,128)(2,1)}, u32[]{:S(2)}) copy-start(bf16[768,768]{1,0:T(8,128)(2,1)} %get-tuple-element.65) | copy-start | bytes 3538948
  213.6 1.7 copy-start.2
  215.3 1.8 copy-start.1
  217.0 2.2 copy-start
